TPU v7x, 32 devices: a whole 2x2x4 slice. The times are simulated.
32 devices in a mesh: patch: 8 (over z, core), visit: 4 (over y, x).
Axes of the slice: x: 2, y: 2, z: 4, core: 2. Of those that a mesh axis runs over, the one named last changes fastest.
Arguments:
- blocks: bfloat16 [8, 4, 16, 256, 256], P('patch', 'visit'), may hold values from -6 to 6
- block_patch: int32 [8, 4, 16, 1], P('patch', 'visit'), may hold values from 0 to 7; in each aligned block of 16 rows (0 to 15, 16 to 31, ..., all dimensions but the last counted through in order) at most 2 rows name the same one
- block_slot: int32 [8, 4, 16], P('patch', 'visit'), may hold values from 0 to 7
- block_count: int32 [8, 4], P('patch', 'visit'), may hold values from 12 to 16, as said below
- template: bfloat16 [8, 512, 1024], P('patch', 'visit'), may hold values from -6 to 6
- basis_rows: bfloat16 [9, 21], replicated, may hold values from -1.25 to 1.25
- basis_cols: float32 [9, 21], replicated, may hold values from -1.25 to 1.25
- coeffs: float32 [4, 9], P('visit'), may hold values from -2 to 2
- psf_rows: bfloat16 [4, 2, 25], P('visit'), may hold values from -1.25 to 1.25
- psf_cols: bfloat16 [4, 2, 25], P('visit'), may hold values from -1.25 to 1.25
Outputs:
- filtered: float32 [8, 4, 512, 1024], P('patch', 'visit')
Inputs may be any that keep to these rules, and one draw needn't show every extreme that they name: `block_patch`: among the 16 entries of one list (one patch index and visit) no patch is named more than 2 times, and some list names a patch exactly 2 times. Entries at positions block_count and beyond are unused.
All inputs are finite; a program needn't handle non-finite values.
Results may differ from a plain program's by a relative error of at most 0.005.
Values may be sent and summed in bfloat16 or wider, within the bound.
A program may use at most 128 MiB of HBM per device.

v0:
```python
import jax
import jax.numpy as jnp
from jax import lax
from jax.sharding import PartitionSpec as P

CAP = 2


def one_hot_bands(length, tile_size):
    band_shape = (3, length, tile_size, tile_size)
    side_ids = lax.broadcasted_iota(jnp.int32, band_shape, 0) - 1
    tap_ids = lax.broadcasted_iota(jnp.int32, band_shape, 1)
    inner = lax.broadcasted_iota(jnp.int32, band_shape, 2)
    outer = lax.broadcasted_iota(jnp.int32, band_shape, 3)
    return (side_ids * tile_size + inner - outer + length // 2 == tap_ids).astype(jnp.float32)


def band_tables(kernel_taps, one_hot):
    return jnp.einsum(
        "cl,dlij->cdij", kernel_taps.astype(jnp.float32), one_hot, precision=lax.Precision.HIGHEST
    ).astype(jnp.bfloat16)


def across_columns(source, tables):
    tile_size = tables.shape[-1]
    height, breadth = source.shape
    tile_count = breadth // tile_size
    tiled = source.reshape(height, tile_count, tile_size)
    zero_block = jnp.zeros((height, 1, tile_size), source.dtype)
    left_side = jnp.concatenate([zero_block, tiled[:, :-1]], axis=1)
    right_side = jnp.concatenate([tiled[:, 1:], zero_block], axis=1)
    summed = jnp.einsum("hbt,ctu->chbu", tiled, tables[:, 1], preferred_element_type=jnp.float32)
    summed = summed + jnp.einsum(
        "hbt,ctu->chbu", left_side, tables[:, 0], preferred_element_type=jnp.float32
    )
    summed = summed + jnp.einsum(
        "hbt,ctu->chbu", right_side, tables[:, 2], preferred_element_type=jnp.float32
    )
    return summed.reshape(tables.shape[0], height, breadth)


def across_rows(source, tables):
    tile_size = tables.shape[-1]
    channels, height, breadth = source.shape
    tile_count = height // tile_size
    tiled = source.reshape(channels, tile_count, tile_size, breadth)
    zero_block = jnp.zeros((channels, 1, tile_size, breadth), source.dtype)
    left_side = jnp.concatenate([zero_block, tiled[:, :-1]], axis=1)
    right_side = jnp.concatenate([tiled[:, 1:], zero_block], axis=1)
    summed = jnp.einsum("cbin,cij->bjn", tiled, tables[:, 1], preferred_element_type=jnp.float32)
    summed = summed + jnp.einsum(
        "cbin,cij->bjn", left_side, tables[:, 0], preferred_element_type=jnp.float32
    )
    summed = summed + jnp.einsum(
        "cbin,cij->bjn", right_side, tables[:, 2], preferred_element_type=jnp.float32
    )
    return summed.reshape(height, breadth)


def place_blocks(
    blocks, block_patch, block_slot, block_count, capacity, slot_total, height, breadth
):
    count_here = blocks.shape[2]
    block_edge = blocks.shape[3]
    pieces = blocks.reshape(count_here, block_edge * block_edge)
    destination = block_patch.reshape(count_here)
    slot_index = block_slot.reshape(count_here)
    row_order = lax.broadcasted_iota(jnp.int32, (count_here, count_here), 0)
    col_order = lax.broadcasted_iota(jnp.int32, (count_here, count_here), 1)
    same_patch = destination[:, None] == destination[None, :]
    earlier = jnp.sum((same_patch & (col_order < row_order)).astype(jnp.int32), axis=1)
    target = destination * capacity + earlier
    live_mask = lax.iota(jnp.int32, count_here) < block_count.reshape(())
    n_patch = lax.axis_size("patch")
    places = n_patch * capacity
    place_ids = lax.broadcasted_iota(jnp.int32, (places, count_here), 0)
    picker = ((place_ids == target[None, :]) & live_mask[None, :]).astype(jnp.float32)
    outgoing = jnp.dot(
        picker.astype(jnp.bfloat16), pieces, preferred_element_type=jnp.float32
    ).astype(jnp.bfloat16)
    outgoing = outgoing.reshape(n_patch, capacity, block_edge * block_edge)
    labels = (
        jnp.dot(
            picker, (slot_index - slot_total).astype(jnp.float32), precision=lax.Precision.HIGHEST
        )
        + slot_total
    )
    labels = labels.astype(jnp.bfloat16).reshape(n_patch, capacity)
    arrived, arrived_slots = (
        lax.all_to_all(outgoing, "patch", split_axis=0, concat_axis=0, tiled=True),
        lax.all_to_all(labels, "patch", split_axis=0, concat_axis=0, tiled=True),
    )
    arrived = arrived.reshape(places, block_edge * block_edge)
    slot_ids = lax.broadcasted_iota(jnp.float32, (slot_total, places), 0)
    chosen = (slot_ids == arrived_slots.reshape(1, places).astype(jnp.float32)).astype(jnp.bfloat16)
    placed = jnp.dot(chosen, arrived, preferred_element_type=jnp.float32)
    tall_count = height // block_edge
    wide_count = breadth // block_edge
    placed = placed.reshape(tall_count, wide_count, block_edge, block_edge).transpose(0, 2, 1, 3)
    return placed.reshape(height, breadth)


def per_device(
    blocks,
    block_patch,
    block_slot,
    block_count,
    template,
    basis_rows,
    basis_cols,
    coeffs,
    psf_rows,
    psf_cols,
):
    local_rows = template.shape[1]
    breadth = template.shape[2]
    height = local_rows * lax.axis_size("visit")
    block_edge = blocks.shape[3]
    slot_total = height // block_edge * (breadth // block_edge)
    science = place_blocks(
        blocks, block_patch, block_slot, block_count, CAP, slot_total, height, breadth
    )
    column_hot = one_hot_bands(basis_rows.shape[1], min(128, breadth))
    row_hot = one_hot_bands(basis_cols.shape[1], min(128, height))
    scaled = (coeffs[0][:, None] * basis_cols).astype(jnp.bfloat16)
    start_image = jnp.zeros((height, breadth), jnp.float32)
    all_tables = band_tables(basis_rows, column_hot)
    partial_rows = across_columns(template[0], all_tables).astype(jnp.bfloat16)
    smoothed_all = lax.all_gather(partial_rows, "visit", axis=1, tiled=True)

    def per_stack(model_image, profiles):
        smoothed, col_taps = profiles
        col_table = band_tables(col_taps[None], row_hot)
        return (model_image + across_rows(smoothed[None], col_table), None)

    model_image = lax.scan(per_stack, start_image, (smoothed_all, scaled))[0]
    difference = (science - model_image).astype(jnp.bfloat16)
    psf_column_hot = one_hot_bands(psf_rows.shape[2], min(128, breadth))
    psf_row_hot = one_hot_bands(psf_cols.shape[2], min(128, height))
    blurred = across_columns(difference, band_tables(psf_rows[0], psf_column_hot)).astype(
        jnp.bfloat16
    )
    filtered = across_rows(blurred, band_tables(psf_cols[0], psf_row_hot))
    return filtered[None, None]


def solution(mesh):
    placed = (
        P("patch", "visit", None, None, None),
        P("patch", "visit", None, None),
        P("patch", "visit", None),
        P("patch", "visit"),
        P("patch", "visit", None),
        P(),
        P(),
        P("visit", None),
        P("visit", None, None),
        P("visit", None, None),
    )
    return jax.shard_map(
        per_device,
        mesh=mesh,
        in_specs=placed,
        out_specs=P("patch", "visit", None, None),
        check_vma=False,
    )
```

profile of v0, /device:TPU:9, one launch (start us, length us, event | category | flops | bytes accessed | tf_op | source)
XLA Modules:
  0.0 236.8 jit_solution(14624126274584516626)
XLA Ops:
  6.5 0.7 copy-done
  7.2 1.4 fusion.36
  8.9 0.7 copy-done.5
  10.2 0.8 fusion.49
  11.0 0.8 fusion.51
  11.8 0.8 add_convert_fusion
  12.6 2.4 %copy.80 = bf16[9,128,1024]{2,1,0:T(8,128)(2,1)} copy(bf16[9,128,1024]{1,2,0:T(8,128)(2,1)S(1)} %bitcast.214) | data formatting | bytes 4718592 | tf_op jit(solution)/shard_map/convert_element_type | solution.py:128
  16.2 0.7 all_to_all.12
  16.9 5.6 %all-to-all-start = ((bf16[8,1,2]{2,1,0:T(2,128)(2,1)}), bf16[8,1,2]{2,1,0:T(2,128)(2,1)S(1)}, u32[]{:S(2)}, u32[]{:S(2)}) async-start(bf16[8,1,2]{2,1,0:T(2,128)(2,1)} %all_to_all.12), calls=%async_computation | async-start | bytes 8192 | tf_op jit(solution)/shard_map/all_to_all | solution.py:91
  22.5 1.2 copy.132
  23.7 0.7 convolution_convert_fusion
  24.3 2.3 reshape.116
  26.7 5.6 %all-to-all-start.1 = ((bf16[8,2,65536]{2,1,0:T(2,128)(2,1)}), bf16[8,2,65536]{2,1,0:T(2,128)(2,1)}, u32[]{:S(2)}, u32[]{:S(2)}) async-start(bf16[8,2,65536]{2,1,0:T(2,128)(2,1)} %reshape.116), calls=%async_computation.1 | async-start | bytes 4194304 | tf_op jit(solution)/shard_map/all_to_all | solution.py:90
  32.3 1.5 fusion.40
  34.5 1.5 fusion.39
  36.2 41.6 %all-to-all-done.1 = bf16[8,2,65536]{2,1,0:T(2,128)(2,1)} async-done(((bf16[8,2,65536]{2,1,0:T(2,128)(2,1)}), bf16[8,2,65536]{2,1,0:T(2,128)(2,1)}, u32[]{:S(2)}, u32[]{:S(2)}) %all-to-all-start.1) | async-done | bytes 2097184 | tf_op jit(solution)/shard_map/all_to_all | solution.py:90
  77.8 2.1 reshape.117
  79.9 0.6 fusion.26
  81.0 1.8 copy.81
  82.8 29.6 %all-gather.2.cloned.1.call-done = bf16[9,512,1024]{2,1,0:T(8,128)(2,1)} async-done(((bf16[9,128,1024]{2,1,0:T(8,128)(2,1)}), bf16[9,512,1024]{2,1,0:T(8,128)(2,1)}) %all-gather.2.cloned.1.call-update) | async-done | bytes 9437200 | tf_op jit(solution)/shard_map/all_gather | solution.py:129
  112.4 97.7 %while.11 = (s32[]{:T(128)}, f32[512,1024]{1,0:T(8,128)}, bf16[9,21]{1,0:T(8,128)(2,1)S(1)}, bf16[9,512,1024]{2,1,0:T(8,128)(2,1)}, s32[3]{0:T(128)S(1)}, /*index=5*/s32[]{:T(128)}, s32[]{:T(128)}) while((s32[]{:T(128)}, f32[512,1024]{1,0:T(8,128)}, bf16[9,21]{1,0:T(8,128)(2,1)S(1)}, bf16[9,512,1024]{2,1,0:T(8,128)(2,1)}, ...), condition=%wide.region_2.3_spmd.clone, body=%wide.region_1.2_spmd.clone.sunk | while | flops 422297600 | bytes 33489512 | solution.py:136
  112.4 0.6 fusion.116
  113.0 4.0 %fusion.117 = bf16[1,3,128,128]{3,0,2,1:T(2,128)(2,1)S(1)} fusion(f32[3,21,128,128]{3,2,1,0:T(8,128)S(1)} %fusion.116, bf16[9,21]{1,0:T(8,128)(2,1)S(1)} %get-tuple-element.132, s32[]{:T(128)} %get-tuple-element.123), kind=kOutput, calls=%fused_computation.1.clone.1 | convolution fusion | flops 12386304 | bytes 4227588 | tf_op jit(solution)/shard_map/while/body/eval_jaxpr/cl,dlij->cdij/dot_general | solution.py:19
  117.1 1.3 constant_dynamic-slice_fusion.2
  119.8 2.0 bitcast_add_fusion.4
  122.4 4.0 %fusion.117 = bf16[1,3,128,128]{3,0,2,1:T(2,128)(2,1)S(1)} fusion(f32[3,21,128,128]{3,2,1,0:T(8,128)S(1)} %fusion.116, bf16[9,21]{1,0:T(8,128)(2,1)S(1)} %get-tuple-element.132, s32[]{:T(128)} %get-tuple-element.123), kind=kOutput, calls=%fused_computation.1.clone.1 | convolution fusion | flops 12386304 | bytes 4227588 | tf_op jit(solution)/shard_map/while/body/eval_jaxpr/cl,dlij->cdij/dot_general | solution.py:19
  126.5 1.3 constant_dynamic-slice_fusion.2
  129.3 3.6 %bitcast_add_fusion.4 = f32[512,1024]{1,0:T(8,128)} fusion(f32[128,4,1024]{2,0,1:T(8,128)S(1)} %add_add_fusion.2, f32[512,1024]{1,0:T(8,128)} %get-tuple-element.124, pred[]{:T(512)S(6)} %compare.11), kind=kLoop, calls=%fused_computation.5.clone.1 | loop fusion | flops 1048576 | bytes 6291457 | tf_op jit(solution)/shard_map/while/body/eval_jaxpr/add | solution.py:134
  132.8 0.6 fusion.116
  133.4 4.0 %fusion.117 = bf16[1,3,128,128]{3,0,2,1:T(2,128)(2,1)S(1)} fusion(f32[3,21,128,128]{3,2,1,0:T(8,128)S(1)} %fusion.116, bf16[9,21]{1,0:T(8,128)(2,1)S(1)} %get-tuple-element.132, s32[]{:T(128)} %get-tuple-element.123), kind=kOutput, calls=%fused_computation.1.clone.1 | convolution fusion | flops 12386304 | bytes 4227588 | tf_op jit(solution)/shard_map/while/body/eval_jaxpr/cl,dlij->cdij/dot_general | solution.py:19
  137.5 1.3 constant_dynamic-slice_fusion.2
  140.3 3.6 %bitcast_add_fusion.4 = f32[512,1024]{1,0:T(8,128)} fusion(f32[128,4,1024]{2,0,1:T(8,128)S(1)} %add_add_fusion.2, f32[512,1024]{1,0:T(8,128)} %get-tuple-element.124, pred[]{:T(512)S(6)} %compare.11), kind=kLoop, calls=%fused_computation.5.clone.1 | loop fusion | flops 1048576 | bytes 6291457 | tf_op jit(solution)/shard_map/while/body/eval_jaxpr/add | solution.py:134
  144.5 4.0 %fusion.117 = bf16[1,3,128,128]{3,0,2,1:T(2,128)(2,1)S(1)} fusion(f32[3,21,128,128]{3,2,1,0:T(8,128)S(1)} %fusion.116, bf16[9,21]{1,0:T(8,128)(2,1)S(1)} %get-tuple-element.132, s32[]{:T(128)} %get-tuple-element.123), kind=kOutput, calls=%fused_computation.1.clone.1 | convolution fusion | flops 12386304 | bytes 4227588 | tf_op jit(solution)/shard_map/while/body/eval_jaxpr/cl,dlij->cdij/dot_general | solution.py:19
  148.6 1.3 constant_dynamic-slice_fusion.2
  151.3 3.6 %bitcast_add_fusion.4 = f32[512,1024]{1,0:T(8,128)} fusion(f32[128,4,1024]{2,0,1:T(8,128)S(1)} %add_add_fusion.2, f32[512,1024]{1,0:T(8,128)} %get-tuple-element.124, pred[]{:T(512)S(6)} %compare.11), kind=kLoop, calls=%fused_computation.5.clone.1 | loop fusion | flops 1048576 | bytes 6291457 | tf_op jit(solution)/shard_map/while/body/eval_jaxpr/add | solution.py:134
  155.5 4.0 %fusion.117 = bf16[1,3,128,128]{3,0,2,1:T(2,128)(2,1)S(1)} fusion(f32[3,21,128,128]{3,2,1,0:T(8,128)S(1)} %fusion.116, bf16[9,21]{1,0:T(8,128)(2,1)S(1)} %get-tuple-element.132, s32[]{:T(128)} %get-tuple-element.123), kind=kOutput, calls=%fused_computation.1.clone.1 | convolution fusion | flops 12386304 | bytes 4227588 | tf_op jit(solution)/shard_map/while/body/eval_jaxpr/cl,dlij->cdij/dot_general | solution.py:19
  159.6 1.3 constant_dynamic-slice_fusion.2
  162.4 3.6 %bitcast_add_fusion.4 = f32[512,1024]{1,0:T(8,128)} fusion(f32[128,4,1024]{2,0,1:T(8,128)S(1)} %add_add_fusion.2, f32[512,1024]{1,0:T(8,128)} %get-tuple-element.124, pred[]{:T(512)S(6)} %compare.11), kind=kLoop, calls=%fused_computation.5.clone.1 | loop fusion | flops 1048576 | bytes 6291457 | tf_op jit(solution)/shard_map/while/body/eval_jaxpr/add | solution.py:134
  166.5 4.0 %fusion.117 = bf16[1,3,128,128]{3,0,2,1:T(2,128)(2,1)S(1)} fusion(f32[3,21,128,128]{3,2,1,0:T(8,128)S(1)} %fusion.116, bf16[9,21]{1,0:T(8,128)(2,1)S(1)} %get-tuple-element.132, s32[]{:T(128)} %get-tuple-element.123), kind=kOutput, calls=%fused_computation.1.clone.1 | convolution fusion | flops 12386304 | bytes 4227588 | tf_op jit(solution)/shard_map/while/body/eval_jaxpr/cl,dlij->cdij/dot_general | solution.py:19
  170.6 1.3 constant_dynamic-slice_fusion.2
  173.4 3.6 %bitcast_add_fusion.4 = f32[512,1024]{1,0:T(8,128)} fusion(f32[128,4,1024]{2,0,1:T(8,128)S(1)} %add_add_fusion.2, f32[512,1024]{1,0:T(8,128)} %get-tuple-element.124, pred[]{:T(512)S(6)} %compare.11), kind=kLoop, calls=%fused_computation.5.clone.1 | loop fusion | flops 1048576 | bytes 6291457 | tf_op jit(solution)/shard_map/while/body/eval_jaxpr/add | solution.py:134
  177.0 0.6 fusion.116
  177.6 4.0 %fusion.117 = bf16[1,3,128,128]{3,0,2,1:T(2,128)(2,1)S(1)} fusion(f32[3,21,128,128]{3,2,1,0:T(8,128)S(1)} %fusion.116, bf16[9,21]{1,0:T(8,128)(2,1)S(1)} %get-tuple-element.132, s32[]{:T(128)} %get-tuple-element.123), kind=kOutput, calls=%fused_computation.1.clone.1 | convolution fusion | flops 12386304 | bytes 4227588 | tf_op jit(solution)/shard_map/while/body/eval_jaxpr/cl,dlij->cdij/dot_general | solution.py:19
  181.7 1.3 constant_dynamic-slice_fusion.2
  184.4 3.6 %bitcast_add_fusion.4 = f32[512,1024]{1,0:T(8,128)} fusion(f32[128,4,1024]{2,0,1:T(8,128)S(1)} %add_add_fusion.2, f32[512,1024]{1,0:T(8,128)} %get-tuple-element.124, pred[]{:T(512)S(6)} %compare.11), kind=kLoop, calls=%fused_computation.5.clone.1 | loop fusion | flops 1048576 | bytes 6291457 | tf_op jit(solution)/shard_map/while/body/eval_jaxpr/add | solution.py:134
  188.0 0.6 fusion.116
  188.6 4.0 %fusion.117 = bf16[1,3,128,128]{3,0,2,1:T(2,128)(2,1)S(1)} fusion(f32[3,21,128,128]{3,2,1,0:T(8,128)S(1)} %fusion.116, bf16[9,21]{1,0:T(8,128)(2,1)S(1)} %get-tuple-element.132, s32[]{:T(128)} %get-tuple-element.123), kind=kOutput, calls=%fused_computation.1.clone.1 | convolution fusion | flops 12386304 | bytes 4227588 | tf_op jit(solution)/shard_map/while/body/eval_jaxpr/cl,dlij->cdij/dot_general | solution.py:19
  192.7 1.3 constant_dynamic-slice_fusion.2
  195.5 3.6 %bitcast_add_fusion.4 = f32[512,1024]{1,0:T(8,128)} fusion(f32[128,4,1024]{2,0,1:T(8,128)S(1)} %add_add_fusion.2, f32[512,1024]{1,0:T(8,128)} %get-tuple-element.124, pred[]{:T(512)S(6)} %compare.11), kind=kLoop, calls=%fused_computation.5.clone.1 | loop fusion | flops 1048576 | bytes 6291457 | tf_op jit(solution)/shard_map/while/body/eval_jaxpr/add | solution.py:134
  199.0 0.6 fusion.116
  199.6 4.0 %fusion.117 = bf16[1,3,128,128]{3,0,2,1:T(2,128)(2,1)S(1)} fusion(f32[3,21,128,128]{3,2,1,0:T(8,128)S(1)} %fusion.116, bf16[9,21]{1,0:T(8,128)(2,1)S(1)} %get-tuple-element.132, s32[]{:T(128)} %get-tuple-element.123), kind=kOutput, calls=%fused_computation.1.clone.1 | convolution fusion | flops 12386304 | bytes 4227588 | tf_op jit(solution)/shard_map/while/body/eval_jaxpr/cl,dlij->cdij/dot_general | solution.py:19
  203.7 1.3 constant_dynamic-slice_fusion.2
  206.5 3.6 %bitcast_add_fusion.4 = f32[512,1024]{1,0:T(8,128)} fusion(f32[128,4,1024]{2,0,1:T(8,128)S(1)} %add_add_fusion.2, f32[512,1024]{1,0:T(8,128)} %get-tuple-element.124, pred[]{:T(512)S(6)} %compare.11), kind=kLoop, calls=%fused_computation.5.clone.1 | loop fusion | flops 1048576 | bytes 6291457 | tf_op jit(solution)/shard_map/while/body/eval_jaxpr/add | solution.py:134
  210.1 3.0 %copy.82 = f32[512,1024]{0,1:T(8,128)} copy(f32[512,1024]{1,0:T(8,128)} %get-tuple-element.32) | data formatting | bytes 4194304 | tf_op jit(solution)/shard_map/while | solution.py:136
  213.1 2.0 subtract_convert_fusion
  215.2 1.1 fusion.93
  216.3 1.5 copy.129
  217.8 1.3 copy.130
  219.1 0.7 fusion.44
  219.8 0.7 fusion.61
  221.0 0.7 fusion.35
  221.7 2.0 convert_element_type.117
  223.7 3.0 %copy.90 = bf16[2,4,128,1024]{3,2,0,1:T(8,128)(2,1)S(1)} copy(bf16[2,4,128,1024]{2,1,3,0:T(4,128)(2,1)} %convert_element_type.117) | data formatting | bytes 4194304 | tf_op jit(solution)/shard_map/convert_element_type | solution.py:140
  228.1 1.9 bitcast_add_fusion.1
  (107 shorter events, 20.7 us)
Async XLA Ops:
  6.5 0.7 copy-start
  6.5 105.8 %all-gather.2.cloned.1.call-start = ((), (), s32[]{:S(2)}) async-start(), calls=%async_computation.2 | async-start | bytes 11796480 | tf_op jit(solution)/shard_map/all_gather | solution.py:129
  8.6 1.0 copy-start.5
  15.0 0.8 copy-start.8
  15.0 1.0 copy-start.9
  15.0 7.5 %copy-start.4 = (bf16[1,1,16,256,256]{4,3,2,1,0:T(8,128)(2,1)S(1)}, bf16[1,1,16,256,256]{4,3,2,1,0:T(8,128)(2,1)}, u32[]{:S(2)}) copy-start(bf16[1,1,16,256,256]{4,3,2,1,0:T(8,128)(2,1)} %param.12) | copy-start | bytes 6291460
  16.9 9.8 %all-to-all-start = ((bf16[8,1,2]{2,1,0:T(2,128)(2,1)}), bf16[8,1,2]{2,1,0:T(2,128)(2,1)S(1)}, u32[]{:S(2)}, u32[]{:S(2)}) async-start(bf16[8,1,2]{2,1,0:T(2,128)(2,1)} %all_to_all.12), calls=%async_computation | async-start | bytes 8192 | tf_op jit(solution)/shard_map/all_to_all | solution.py:91
  26.7 5.6 %copy-start.10 = (bf16[1,2,25]{2,1,0:T(2,128)(2,1)S(1)}, bf16[1,2,25]{2,1,0:T(2,128)(2,1)}, u32[]{:S(2)}) copy-start(bf16[1,2,25]{2,1,0:T(2,128)(2,1)} %param.21) | copy-start | bytes 304
  26.7 51.2 %all-to-all-start.1 = ((bf16[8,2,65536]{2,1,0:T(2,128)(2,1)}), bf16[8,2,65536]{2,1,0:T(2,128)(2,1)}, u32[]{:S(2)}, u32[]{:S(2)}) async-start(bf16[8,2,65536]{2,1,0:T(2,128)(2,1)} %reshape.116), calls=%async_computation.1 | async-start | bytes 4194304 | tf_op jit(solution)/shard_map/all_to_all | solution.py:90
  32.3 2.1 copy-start.6
  32.3 2.1 copy-start.7
  32.3 2.1 copy-start.11
  210.1 3.0 %copy-start.2 = (f32[512,1024]{0,1:T(8,128)S(1)}, f32[512,1024]{0,1:T(8,128)}, u32[]{:S(2)}) copy-start(f32[512,1024]{0,1:T(8,128)} %copy.81) | copy-start | bytes 6291460
  219.8 1.2 copy-start.3
  228.1 1.9 copy-start.1
Sparse Core Ops, SparseCore 0:
  15.1 97.1 all-gather.1
where the time goes:
time: 240 us; the launch traced here: 237 us
  waiting for transfers between devices  71.2 us (30%)
  matrix products  59.7 us (25%)
  local copies, waits for them, and re-layouts  41.5 us (17%)
  other arithmetic  38.2 us (16%)
  between operations  14.5 us (6%)
  starting transfers between devices  11.2 us (5%)
    all_to_all x1, waiting for transfers between devices, place_blocks(): lax.all_to_all(outgoing, 'patch', split_axis=0, concat_axis=0, tiled=True)  41.6 us
    dot_general x12, matrix products, band_tables(): jnp.einsum('cl,dlij->cdij', kernel_taps.astype(jnp.float32), one_hot, pre...  39.9 us
    add x9, other arithmetic, per_stack(): return (model_image + across_rows(smoothed[None], col_table), None)  30.6 us
    all_gather x1, waiting for transfers between devices, per_device(): smoothed_all = lax.all_gather(partial_rows, 'visit', axis=1, tiled=True)  29.6 us
    dynamic_slice x9, local copies, waits for them, and re-layouts, per_device(): model_image = lax.scan(per_stack, start_image, (smoothed_all, scaled))[0]  11.7 us
    unnamed x31, local copies, waits for them, and re-layouts  6.84 us
    all_to_all x1, starting transfers between devices, place_blocks(): lax.all_to_all(outgoing, 'patch', split_axis=0, concat_axis=0, tiled=True)  5.63 us
    all_to_all x1, starting transfers between devices, place_blocks(): lax.all_to_all(labels, 'patch', split_axis=0, concat_axis=0, tiled=True)  5.6 us
  transfers between devices with their start and end apart: 3, of which 2 were waited for; matrix products, arithmetic and copies ran while one was open for 6% of the time, Pallas kernels for 0%

commit v1 on v0

v1 whole, which is shorter than its diff:
```python
import functools

import jax
import jax.numpy as jnp
from jax import lax
from jax.experimental import pallas as pl
from jax.experimental.pallas import tpu as pltpu
from jax.sharding import PartitionSpec as P

CAP = 2
LANE = 128
HALF = 64
WIN = 256
F32 = jnp.float32
BF16 = jnp.bfloat16
VMEM_LIMIT = 56 * 1024 * 1024


def column_table(row, half_len):
    wide = jnp.broadcast_to(row, (WIN, WIN))
    return pltpu.roll(wide, (WIN - HALF - half_len) // 8 * 8, 1, stride=1, stride_axis=0)[:, :LANE].astype(BF16)


def row_table(row, half_len):
    wide = jnp.broadcast_to(row, (LANE, WIN))
    return pltpu.roll(wide, (HALF - half_len) // 8 * 8, 1, stride=1, stride_axis=0).astype(BF16)


def shift_into(load_tile, shifted, height, tiles, step):
    def body(r, carry):
        rows = pl.ds(pl.multiple_of(r * step, step), step)
        lane = lax.broadcasted_iota(jnp.int32, (step, LANE), 1)
        before = jnp.zeros((step, LANE), F32)
        for t in range(tiles):
            rolled = pltpu.roll(load_tile(rows, t), HALF, 1)
            shifted[rows, t * LANE : (t + 1) * LANE] = jnp.where(lane < HALF, before, rolled).astype(BF16)
            before = rolled
        shifted[rows, tiles * LANE :] = jnp.where(lane < HALF, before, 0.0).astype(BF16)
        return carry

    lax.fori_loop(0, height // step, body, 0)


def columns_pass(shifted, tables, smooth, pair, count, height):
    for side in range(2):
        start = pl.multiple_of((2 * pair + side) * LANE, LANE)
        window = shifted[:, pl.ds(start, WIN)]
        for group in range(0, count, 2):
            taken = min(2, count - group)
            got = jnp.dot(
                window, tables[:, group * LANE : (group + taken) * LANE], preferred_element_type=F32
            ).astype(BF16)
            for k in range(taken):
                smooth[group + k, HALF : HALF + height, side * LANE : (side + 1) * LANE] = got[
                    :, k * LANE : (k + 1) * LANE
                ]


def rows_pass(smooth, tables, count, r):
    start = pl.multiple_of(r * LANE, LANE)
    total = jnp.zeros((LANE, WIN), F32)
    for k in range(count):
        total = total + jnp.dot(tables[k], smooth[k, pl.ds(start, WIN), :], preferred_element_type=F32)
    return total


def build_tables(column_rows, row_rows, column_tables, row_tables, count, half_c, half_r):
    for k in range(count):
        column_tables[:, k * LANE : (k + 1) * LANE] = column_table(column_rows[k : k + 1, :], half_c)
        row_tables[k] = row_table(row_rows[k : k + 1, :], half_r)


def clear_edges(smooth, count, height):
    for k in range(count):
        smooth[k, :HALF, :] = jnp.zeros((HALF, smooth.shape[2]), BF16)
        smooth[k, HALF + height :, :] = jnp.zeros((HALF, smooth.shape[2]), BF16)


def pack_kernel(places, patch, slot, count, blocks, out, labels, source, named, sems):
    entries = patch.shape[0]

    def reset(d, carry):
        source[d] = 0
        labels[d] = -1
        named[d] = 0
        return carry

    lax.fori_loop(0, places, reset, 0)
    live = count[0]

    def enter(i, carry):
        target = patch[i]
        earlier = named[target]
        named[target] = earlier + 1
        place = target * CAP + earlier

        @pl.when(i < live)
        def _():
            source[place] = i
            labels[place] = slot[i]

        return carry

    lax.fori_loop(0, entries, enter, 0)
    for d in range(places):
        pltpu.make_async_copy(blocks.at[source[d]], out.at[d], sems.at[d]).start()
    for d in range(places):
        pltpu.make_async_copy(blocks.at[0], out.at[d], sems.at[d]).wait()


def model_kernel(halves, template, column_rows, row_rows, model, shifted, column_tables, row_tables, smooth):
    height, breadth = template.shape
    count = column_rows.shape[0]
    build_tables(column_rows, row_rows, column_tables, row_tables, count, *halves)
    clear_edges(smooth, count, height)
    shift_into(
        lambda rows, t: template[rows, t * LANE : (t + 1) * LANE].astype(F32),
        shifted, height, breadth // LANE, 32,
    )

    def per_pair(pair, carry):
        columns_pass(shifted, column_tables, smooth, pair, count, height)

        def per_row(r, inner):
            rows = pl.ds(pl.multiple_of(r * LANE, LANE), LANE)
            columns = pl.ds(pl.multiple_of(pair * WIN, WIN), WIN)
            model[rows, columns] = rows_pass(smooth, row_tables, count, r)
            return inner

        return lax.fori_loop(0, height // LANE, per_row, carry)

    lax.fori_loop(0, breadth // WIN, per_pair, 0)


def final_kernel(halves, labels, arrived, model, column_rows, row_rows, out, total, shifted, column_tables, row_tables, smooth):
    height, breadth = model.shape
    edge = arrived.shape[1]
    wide = breadth // edge
    places = arrived.shape[0]
    count = column_rows.shape[0]
    build_tables(column_rows, row_rows, column_tables, row_tables, count, *halves)
    clear_edges(smooth, count, height)
    total[...] = jnp.zeros(total.shape, F32)

    def add(j, carry):
        s = labels[j]

        @pl.when(s >= 0)
        def _():
            total[s] = total[s] + arrived[j].astype(F32)

        return carry

    lax.fori_loop(0, places, add, 0)
    step = 32
    per_edge = edge // step

    def body(r, carry):
        rows = pl.ds(pl.multiple_of(r * step, step), step)
        tall = r // per_edge
        inside = pl.ds(pl.multiple_of((r % per_edge) * step, step), step)
        lane = lax.broadcasted_iota(jnp.int32, (step, LANE), 1)
        before = jnp.zeros((step, LANE), F32)
        tiles = breadth // LANE
        for t in range(tiles):
            at = t * LANE % edge
            tile = total[tall * wide + t * LANE // edge, inside, at : at + LANE] - model[rows, t * LANE : (t + 1) * LANE]
            rolled = pltpu.roll(tile, HALF, 1)
            shifted[rows, t * LANE : (t + 1) * LANE] = jnp.where(lane < HALF, before, rolled).astype(BF16)
            before = rolled
        shifted[rows, tiles * LANE :] = jnp.where(lane < HALF, before, 0.0).astype(BF16)
        return carry

    lax.fori_loop(0, height // step, body, 0)

    def per_pair(pair, carry):
        columns_pass(shifted, column_tables, smooth, pair, count, height)

        def per_row(r, inner):
            rows = pl.ds(pl.multiple_of(r * LANE, LANE), LANE)
            columns = pl.ds(pl.multiple_of(pair * WIN, WIN), WIN)
            out[rows, columns] = rows_pass(smooth, row_tables, count, r)
            return inner

        return lax.fori_loop(0, height // LANE, per_row, carry)

    lax.fori_loop(0, breadth // WIN, per_pair, 0)


def padded(taps, flip):
    taps = taps.astype(F32)
    if flip:
        taps = taps[:, ::-1]
    lead = (HALF - taps.shape[1] // 2) % 8
    return jnp.pad(taps, ((0, 0), (lead, WIN - lead - taps.shape[1])))


SMEM = pl.BlockSpec(memory_space=pltpu.SMEM)
VMEM = pl.BlockSpec(memory_space=pltpu.VMEM)
ANY = pl.BlockSpec(memory_space=pl.ANY)


def stencil_scratch(count, height, breadth):
    return [
        pltpu.VMEM((height, breadth + LANE), BF16),
        pltpu.VMEM((WIN, count * LANE), BF16),
        pltpu.VMEM((count, LANE, WIN), BF16),
        pltpu.VMEM((count, height + 2 * HALF, WIN), BF16),
    ]


def per_device(blocks, block_patch, block_slot, block_count, template, basis_rows, basis_cols, coeffs, psf_rows, psf_cols):
    n_patch = lax.axis_size("patch")
    n_visit = lax.axis_size("visit")
    local_rows, breadth = template.shape[1:]
    height = local_rows * n_visit
    entries, edge = blocks.shape[2:4]
    places = n_patch * CAP
    slots = height // edge * (breadth // edge)
    outgoing, labels = pl.pallas_call(
        functools.partial(pack_kernel, places),
        out_shape=(
            jax.ShapeDtypeStruct((places, edge, edge), BF16),
            jax.ShapeDtypeStruct((places,), jnp.int32),
        ),
        in_specs=[SMEM, SMEM, SMEM, ANY],
        out_specs=(ANY, SMEM),
        scratch_shapes=[
            pltpu.SMEM((places,), jnp.int32),
            pltpu.SMEM((places,), jnp.int32),
            pltpu.SemaphoreType.DMA((places,)),
        ],
    )(block_patch.reshape(entries), block_slot.reshape(entries), block_count.reshape(1), blocks[0, 0])
    arrived = lax.all_to_all(outgoing, "patch", split_axis=0, concat_axis=0, tiled=True)
    arrived_labels = lax.all_to_all(labels, "patch", split_axis=0, concat_axis=0, tiled=True)
    scaled = (coeffs[0][:, None] * basis_cols).astype(BF16)
    me = lax.axis_index("visit")
    whole = jnp.zeros((height, breadth), BF16)
    whole = lax.dynamic_update_slice(whole, template[0], (me * local_rows, 0))
    for hop in range(1, n_visit):
        moved = lax.ppermute(template[0], "visit", [(d, (d + hop) % n_visit) for d in range(n_visit)])
        whole = lax.dynamic_update_slice(whole, moved, ((me + n_visit - hop) % n_visit * local_rows, 0))
    params = pltpu.CompilerParams(vmem_limit_bytes=VMEM_LIMIT)
    model = pl.pallas_call(
        functools.partial(model_kernel, (basis_rows.shape[1] // 2, basis_cols.shape[1] // 2)),
        out_shape=jax.ShapeDtypeStruct((height, breadth), F32),
        in_specs=[VMEM] * 3,
        out_specs=VMEM,
        scratch_shapes=stencil_scratch(basis_rows.shape[0], height, breadth),
        compiler_params=params,
        cost_estimate=pl.CostEstimate(flops=20_000_000_000, bytes_accessed=4 * height * breadth, transcendentals=0),
    )(whole, padded(basis_rows, True), padded(scaled, False))
    filtered = pl.pallas_call(
        functools.partial(final_kernel, (psf_rows.shape[2] // 2, psf_cols.shape[2] // 2)),
        out_shape=jax.ShapeDtypeStruct((height, breadth), F32),
        in_specs=[SMEM] + [VMEM] * 4,
        out_specs=VMEM,
        scratch_shapes=[pltpu.VMEM((slots, edge, edge), F32)] + stencil_scratch(psf_rows.shape[1], height, breadth),
        compiler_params=params,
    )(arrived_labels, arrived, model, padded(psf_rows[0], True), padded(psf_cols[0], False))
    return filtered[None, None]


def solution(mesh):
    return jax.shard_map(
        per_device,
        mesh=mesh,
        in_specs=(
            P("patch", "visit", None, None, None),
            P("patch", "visit", None, None),
            P("patch", "visit", None),
            P("patch", "visit"),
            P("patch", "visit", None),
            P(),
            P(),
            P("visit", None),
            P("visit", None, None),
            P("visit", None, None),
        ),
        out_specs=P("patch", "visit", None, None),
        check_vma=False,
    )
```

time: 240 us -> 144 us (0.60)
  the two profiles are of different devices: /device:TPU:9 before, /device:TPU:0 now
where the time goes in v1:
time: 144 us
  Pallas kernels  89.5 us (62%)
  waiting for transfers between devices  22.5 us (16%)
  blocking collectives  11.7 us (8%)
  local copies, waits for them, and re-layouts  8.78 us (6%)
  starting transfers between devices  8.24 us (6%)
  other arithmetic  2.04 us (1%)
    pallas_call x1, Pallas kernels, per_device(): pl.pallas_call(functools.partial(pack_kernel, places), out_shape=(jax.Sha...  66.3 us
    all_to_all x1, waiting for transfers between devices, per_device(): lax.all_to_all(outgoing, 'patch', split_axis=0, concat_axis=0, tiled=True)  17.7 us
    pallas_call x1, Pallas kernels, per_device(): pl.pallas_call(functools.partial(model_kernel, (basis_rows.shape[1] // 2,...  13.1 us
    all_to_all x1, blocking collectives, per_device(): lax.all_to_all(labels, 'patch', split_axis=0, concat_axis=0, tiled=True)  11.7 us
    pallas_call x1, Pallas kernels, per_device(): pl.pallas_call(functools.partial(final_kernel, (psf_rows.shape[2] // 2, p...  10.1 us
    ppermute x3, waiting for transfers between devices, per_device(): lax.ppermute(template[0], 'visit', [(d, (d + hop) % n_visit) for d in ran...  4.82 us
    ppermute x3, starting transfers between devices, per_device(): lax.ppermute(template[0], 'visit', [(d, (d + hop) % n_visit) for d in ran...  4.5 us
    all_to_all x1, starting transfers between devices, per_device(): lax.all_to_all(outgoing, 'patch', split_axis=0, concat_axis=0, tiled=True)  3.75 us
  transfers between devices with their start and end apart: 4, of which 3 were waited for; matrix products, arithmetic and copies ran while one was open for 5% of the time, Pallas kernels for 9%

profile of v1, /device:TPU:0, one launch (start us, length us, event | category | flops | bytes accessed | tf_op | source)
XLA Modules:
  0.0 143.6 jit_solution(17753527260253563176)
XLA Ops:
  0.7 66.3 %shard_map.100 = (bf16[16,256,256]{2,1,0:T(8,128)(2,1)}, s32[16]{0:T(128)}) custom-call(s32[16]{0:T(128)} %bitcast.20, s32[16]{0:T(128)} %bitcast.21, s32[1]{0:T(128)} %bitcast.14.count, bf16[16,256,256]{2,1,0:T(8,128)(2,1)} %bitcast.15), custom_call_target="tpu_custom_call" | custom-call | tf_op jit(solution)/shard_map/pallas_call | solution.py:220
  67.0 0.7 all_to_all.10
  67.7 11.7 %all_to_all.16 = s32[8,2,1]{1,2,0:T(1,128)S(1)} all-to-all(s32[8,2,1]{1,2,0:T(1,128)S(1)} %bitcast.19), channel_id=1, replica_groups=mesh['patch'=8,'visit'=4] {'patch'}, dimensions={0} | all-to-all | bytes 128 | tf_op jit(solution)/shard_map/all_to_all | solution.py:235
  79.4 0.0 copy-start.2
  79.4 0.0 copy-start.3
  79.4 0.0 copy-start.5
  79.4 0.0 copy-start.7
  79.4 0.0 copy-start.6
  79.4 0.0 copy-start.4
  79.4 3.7 %all-to-all-start.1 = ((bf16[16,256,256]{2,1,0:T(8,128)(2,1)}), bf16[16,256,256]{2,1,0:T(8,128)(2,1)S(1)}, u32[]{:S(2)}, u32[]{:S(2)}) async-start(bf16[16,256,256]{2,1,0:T(8,128)(2,1)} %get-tuple-element.8), calls=%async_computation.1 | async-start | bytes 4194304 | tf_op jit(solution)/shard_map/all_to_all | solution.py:234
  83.2 0.0 copy-done.2
  83.2 1.5 %collective-permute-start = (bf16[128,1024]{1,0:T(8,128)(2,1)S(1)}, bf16[128,1024]{1,0:T(8,128)(2,1)}, u32[]{:S(2)}, u32[]{:S(2)}) collective-permute-start(bf16[128,1024]{1,0:T(8,128)(2,1)S(1)} %bitcast.16), channel_id=1, source_target_pairs={{0,1},{1,2},{2,3},{3,0},{4,5},{5,6},{6,7},{7,4},{8,9},{9,10},{10,1... | collective-permute-start | bytes 786440 | tf_op jit(solution)/shard_map/ppermute | solution.py:241
  84.7 1.5 %collective-permute-start.1 = (bf16[128,1024]{1,0:T(8,128)(2,1)S(1)}, bf16[128,1024]{1,0:T(8,128)(2,1)}, u32[]{:S(2)}, u32[]{:S(2)}) collective-permute-start(bf16[128,1024]{1,0:T(8,128)(2,1)S(1)} %bitcast.17), channel_id=1, source_target_pairs={{0,2},{1,3},{2,0},{3,1},{4,6},{5,7},{6,4},{7,5},{8,10},{9,11},{10,... | collective-permute-start | bytes 786440 | tf_op jit(solution)/shard_map/ppermute | solution.py:241
  86.2 1.4 collective-permute-start.2
  87.7 0.0 copy-done.3
  87.7 0.0 copy-done.5
  87.7 0.1 multiply_convert_fusion
  87.8 0.1 broadcast_in_dim.6
  87.9 0.0 copy-done.7
  87.9 0.7 pad_convert_fusion.row_rows
  88.6 0.0 copy-done.6
  88.6 0.7 pad_convert_fusion.1.row_rows
  89.3 0.0 copy-done.4
  89.3 0.1 rev.6
  89.4 0.1 rev.7
  89.5 0.7 pad.18.column_rows
  90.1 0.7 pad.21.column_rows
  90.8 0.5 broadcast.14
  91.3 0.6 reduce.3
  92.0 0.7 all_to_all.12.labels
  92.6 0.8 collective-permute-done
  93.5 1.0 constant_dynamic-update-slice_fusion.2
  94.4 4.0 %collective-permute-done.1 = bf16[128,1024]{1,0:T(8,128)(2,1)} collective-permute-done((bf16[128,1024]{1,0:T(8,128)(2,1)S(1)}, bf16[128,1024]{1,0:T(8,128)(2,1)}, u32[]{:S(2)}, u32[]{:S(2)}) %collective-permute-start.1) | collective-permute-done | bytes 262176 | tf_op jit(solution)/shard_map/ppermute | solution.py:241
  98.4 1.0 constant_dynamic-update-slice_fusion.1
  99.4 0.0 collective-permute-done.2
  99.4 1.0 constant_dynamic-update-slice_fusion.template
  100.4 0.0 copy-start.1
  100.4 1.0 copy-done.1
  101.4 13.1 %shard_map.101.model = f32[512,1024]{1,0:T(8,128)} custom-call(bf16[512,1024]{1,0:T(8,128)(2,1)} %copy-done.1, f32[9,256]{1,0:T(8,128)} %pad.18.column_rows, f32[9,256]{1,0:T(8,128)} %pad_convert_fusion.row_rows), custom_call_target="tpu_custom_call" | custom-call | flops 20000000000 | bytes 2097152 | tf_op jit(solution)/shard_map/pallas_call | solution.py:244
  114.4 17.7 %all-to-all-done.1.arrived = bf16[16,256,256]{2,1,0:T(8,128)(2,1)S(1)} async-done(((bf16[16,256,256]{2,1,0:T(8,128)(2,1)}), bf16[16,256,256]{2,1,0:T(8,128)(2,1)S(1)}, u32[]{:S(2)}, u32[]{:S(2)}) %all-to-all-start.1) | async-done | bytes 2097184 | tf_op jit(solution)/shard_map/all_to_all | solution.py:234
  132.1 0.0 copy-start
  132.1 1.3 copy-done
  133.5 10.1 %shard_map.102 = f32[512,1024]{1,0:T(8,128)} custom-call(s32[16]{0:T(128)} %all_to_all.12.labels, bf16[16,256,256]{2,1,0:T(8,128)(2,1)} %copy-done, f32[512,1024]{1,0:T(8,128)} %shard_map.101.model, f32[2,256]{1,0:T(2,128)} %pad.21.column_rows, f32[2,256]{1,0:T(2,128)} %pad_convert_fusion.1.row_rows), custom_call_target="tpu_custom_call" | custom-call | tf_op jit(solution)/shard_map/pallas_call | solution.py:253
  (2 shorter events, 0.0 us)
Async XLA Ops:
  79.4 3.8 %copy-start.2 = (bf16[1,128,1024]{2,1,0:T(8,128)(2,1)S(1)}, bf16[1,128,1024]{2,1,0:T(8,128)(2,1)}, u32[]{:S(2)}) copy-start(bf16[1,128,1024]{2,1,0:T(8,128)(2,1)} %param.14) | copy-start | bytes 786436
  79.4 8.3 %copy-start.3 = (f32[9,21]{1,0:T(8,128)S(1)}, f32[9,21]{1,0:T(8,128)}, u32[]{:S(2)}) copy-start(f32[9,21]{1,0:T(8,128)} %param.16) | copy-start | bytes 2272
  79.4 8.3 %copy-start.5 = (f32[1,9]{1,0:T(1,128)S(1)}, f32[1,9]{1,0:T(1,128)}, u32[]{:S(2)}) copy-start(f32[1,9]{1,0:T(1,128)} %param.17) | copy-start | bytes 112
  79.4 8.5 %copy-start.7 = (bf16[1,2,25]{2,1,0:T(2,128)(2,1)S(1)}, bf16[1,2,25]{2,1,0:T(2,128)(2,1)}, u32[]{:S(2)}) copy-start(bf16[1,2,25]{2,1,0:T(2,128)(2,1)} %param.18) | copy-start | bytes 304
  79.4 9.2 %copy-start.6 = (bf16[1,2,25]{2,1,0:T(2,128)(2,1)S(1)}, bf16[1,2,25]{2,1,0:T(2,128)(2,1)}, u32[]{:S(2)}) copy-start(bf16[1,2,25]{2,1,0:T(2,128)(2,1)} %param.19) | copy-start | bytes 304
  79.4 9.9 %copy-start.4 = (bf16[9,21]{1,0:T(8,128)(2,1)S(1)}, bf16[9,21]{1,0:T(8,128)(2,1)}, u32[]{:S(2)}) copy-start(bf16[9,21]{1,0:T(8,128)(2,1)} %param.15) | copy-start | bytes 1138
  79.4 52.7 %all-to-all-start.1 = ((bf16[16,256,256]{2,1,0:T(8,128)(2,1)}), bf16[16,256,256]{2,1,0:T(8,128)(2,1)S(1)}, u32[]{:S(2)}, u32[]{:S(2)}) async-start(bf16[16,256,256]{2,1,0:T(8,128)(2,1)} %get-tuple-element.8), calls=%async_computation.1 | async-start | bytes 4194304 | tf_op jit(solution)/shard_map/all_to_all | solution.py:234
  83.2 10.3 %collective-permute-start = (bf16[128,1024]{1,0:T(8,128)(2,1)S(1)}, bf16[128,1024]{1,0:T(8,128)(2,1)}, u32[]{:S(2)}, u32[]{:S(2)}) collective-permute-start(bf16[128,1024]{1,0:T(8,128)(2,1)S(1)} %bitcast.16), channel_id=1, source_target_pairs={{0,1},{1,2},{2,3},{3,0},{4,5},{5,6},{6,7},{7,4},{8,9},{9,10},{10,1... | collective-permute-start | bytes 786440 | tf_op jit(solution)/shard_map/ppermute | solution.py:241
  84.7 13.7 %collective-permute-start.1 = (bf16[128,1024]{1,0:T(8,128)(2,1)S(1)}, bf16[128,1024]{1,0:T(8,128)(2,1)}, u32[]{:S(2)}, u32[]{:S(2)}) collective-permute-start(bf16[128,1024]{1,0:T(8,128)(2,1)S(1)} %bitcast.17), channel_id=1, source_target_pairs={{0,2},{1,3},{2,0},{3,1},{4,6},{5,7},{6,4},{7,5},{8,10},{9,11},{10,... | collective-permute-start | bytes 786440 | tf_op jit(solution)/shard_map/ppermute | solution.py:241
  86.2 13.1 %collective-permute-start.2 = (bf16[128,1024]{1,0:T(8,128)(2,1)S(1)}, bf16[128,1024]{1,0:T(8,128)(2,1)}, u32[]{:S(2)}, u32[]{:S(2)}) collective-permute-start(bf16[128,1024]{1,0:T(8,128)(2,1)S(1)} %bitcast.18), channel_id=1, source_target_pairs={{0,3},{1,0},{2,1},{3,2},{4,7},{5,4},{6,5},{7,6},{8,11},{9,8},{10,9... | collective-permute-start | bytes 786440 | tf_op jit(solution)/shard_map/ppermute | solution.py:241
  100.4 1.0 copy-start.1
  132.1 1.3 copy-start

commit v2 on v1

v2 whole, which is shorter than its diff:
```python
import functools

import jax
import jax.numpy as jnp
from jax import lax
from jax.experimental import pallas as pl
from jax.experimental.pallas import tpu as pltpu
from jax.sharding import PartitionSpec as P

CAP = 2
LANE = 128
HALF = 64
WIN = 256
F32 = jnp.float32
BF16 = jnp.bfloat16
VMEM_LIMIT = 56 * 1024 * 1024


def column_table(row, half_len):
    wide = jnp.broadcast_to(row, (WIN, WIN))
    return pltpu.roll(wide, (WIN - HALF - half_len) // 8 * 8, 1, stride=1, stride_axis=0)[:, :LANE].astype(BF16)


def row_table(row, half_len):
    wide = jnp.broadcast_to(row, (LANE, WIN))
    return pltpu.roll(wide, (HALF - half_len) // 8 * 8, 1, stride=1, stride_axis=0).astype(BF16)


def shift_into(load_tile, shifted, height, tiles, step):
    def body(r, carry):
        rows = pl.ds(pl.multiple_of(r * step, step), step)
        lane = lax.broadcasted_iota(jnp.int32, (step, LANE), 1)
        before = jnp.zeros((step, LANE), F32)
        for t in range(tiles):
            rolled = pltpu.roll(load_tile(rows, t), HALF, 1)
            shifted[rows, t * LANE : (t + 1) * LANE] = jnp.where(lane < HALF, before, rolled).astype(BF16)
            before = rolled
        shifted[rows, tiles * LANE :] = jnp.where(lane < HALF, before, 0.0).astype(BF16)
        return carry

    lax.fori_loop(0, height // step, body, 0)


def columns_pass(shifted, tables, smooth, pair, count, height):
    for side in range(2):
        start = pl.multiple_of((2 * pair + side) * LANE, LANE)
        window = shifted[:, pl.ds(start, WIN)]
        for group in range(0, count, 2):
            taken = min(2, count - group)
            got = jnp.dot(
                window, tables[:, group * LANE : (group + taken) * LANE], preferred_element_type=F32
            ).astype(BF16)
            for k in range(taken):
                smooth[group + k, HALF : HALF + height, side * LANE : (side + 1) * LANE] = got[
                    :, k * LANE : (k + 1) * LANE
                ]


def rows_pass(smooth, tables, count, r):
    start = pl.multiple_of(r * LANE, LANE)
    total = jnp.zeros((LANE, WIN), F32)
    for k in range(count):
        total = total + jnp.dot(tables[k], smooth[k, pl.ds(start, WIN), :], preferred_element_type=F32)
    return total


def build_tables(column_rows, row_rows, column_tables, row_tables, count, half_c, half_r):
    for k in range(count):
        column_tables[:, k * LANE : (k + 1) * LANE] = column_table(column_rows[k : k + 1, :], half_c)
        row_tables[k] = row_table(row_rows[k : k + 1, :], half_r)


def clear_edges(smooth, count, height):
    for k in range(count):
        smooth[k, :HALF, :] = jnp.zeros((HALF, smooth.shape[2]), BF16)
        smooth[k, HALF + height :, :] = jnp.zeros((HALF, smooth.shape[2]), BF16)


def exchange_kernel(
    n_patch, n_visit, halves,
    patch, slot, live, blocks, template, column_rows, row_rows,
    difference,
    raw, outgoing, arrived, labels_out, labels_in, whole, total, shifted, column_tables, row_tables, smooth,
    load_sem, own_sem, block_send, block_recv, label_send, label_recv, rows_send, rows_recv,
):
    me = lax.axis_index("patch")
    my_visit = lax.axis_index("visit")
    local_rows, breadth = template.shape
    height = local_rows * n_visit
    entries, edge = blocks.shape[:2]
    count = column_rows.shape[0]
    wide = breadth // edge
    turn = 1 - 2 * (me // (n_patch // 2))
    peers = [lax.rem(me + turn * hop + n_patch, n_patch) for hop in range(1, n_patch)]
    visits = [lax.rem(my_visit + hop, n_visit) for hop in range(1, n_visit)]

    load = pltpu.make_async_copy(blocks, raw, load_sem)
    load.start()
    my_rows = pl.ds(pl.multiple_of(my_visit * local_rows, local_rows), local_rows)
    own = pltpu.make_async_copy(template, whole.at[my_rows], own_sem)
    own.start()
    barrier = pltpu.get_barrier_semaphore()
    for peer in peers:
        pl.semaphore_signal(barrier, inc=1, device_id={"patch": peer}, device_id_type=pl.DeviceIdType.MESH)
    for visit in visits:
        pl.semaphore_signal(barrier, inc=1, device_id={"visit": visit}, device_id_type=pl.DeviceIdType.MESH)

    targets = [patch[i] for i in range(entries)]
    place_of = []
    for i in range(entries):
        earlier = jnp.int32(0)
        for before in range(i):
            earlier = earlier + jnp.where(targets[before] == targets[i], 1, 0)
        place_of.append(targets[i] * CAP + earlier)
    marks = [jnp.where(i < live[0], slot[i] + 1, 0) for i in range(entries)]
    load.wait()

    def pack(d, carry):
        source = jnp.int32(0)
        label = jnp.int32(-1)
        for i in range(entries):
            source = source + jnp.where(place_of[i] == d, i, 0)
            label = label + jnp.where(place_of[i] == d, marks[i], 0)
        outgoing[d] = raw[source]
        labels_out[d] = jnp.full((8, LANE), label, jnp.int32)
        return carry

    lax.fori_loop(0, n_patch * CAP, pack, 0)
    pl.semaphore_wait(barrier, n_patch + n_visit - 2)

    row_copies = []
    for hop, visit in enumerate(visits):
        row_copies.append(
            pltpu.make_async_remote_copy(
                src_ref=template, dst_ref=whole.at[my_rows],
                send_sem=rows_send.at[hop], recv_sem=rows_recv.at[my_visit],
                device_id={"visit": visit}, device_id_type=pl.DeviceIdType.MESH,
            )
        )
    copies = []
    for hop, peer in enumerate(peers):
        theirs = pl.ds(peer * CAP, CAP)
        mine = pl.ds(me * CAP, CAP)
        for source, target, send, recv in (
            (labels_out, labels_in, label_send, label_recv),
            (outgoing, arrived, block_send, block_recv),
        ):
            copies.append(
                pltpu.make_async_remote_copy(
                    src_ref=source.at[theirs], dst_ref=target.at[mine],
                    send_sem=send.at[hop], recv_sem=recv.at[me],
                    device_id={"patch": peer}, device_id_type=pl.DeviceIdType.MESH,
                )
            )
    for copy in row_copies:
        copy.start()
    for copy in copies:
        copy.start()

    build_tables(column_rows, row_rows, column_tables, row_tables, count, *halves)
    clear_edges(smooth, count, height)
    own.wait()
    for visit in visits:
        rows = pl.ds(pl.multiple_of(visit * local_rows, local_rows), local_rows)
        pltpu.make_async_copy(whole.at[rows], whole.at[rows], rows_recv.at[visit]).wait()
    shift_into(
        lambda rows, t: whole[rows, t * LANE : (t + 1) * LANE].astype(F32),
        shifted, height, breadth // LANE, 32,
    )

    def per_pair(pair, carry):
        columns_pass(shifted, column_tables, smooth, pair, count, height)

        def per_row(r, inner):
            rows = pl.ds(pl.multiple_of(r * LANE, LANE), LANE)
            columns = pl.ds(pl.multiple_of(pair * WIN, WIN), WIN)
            total[rows, columns] = -rows_pass(smooth, row_tables, count, r)
            return inner

        return lax.fori_loop(0, height // LANE, per_row, carry)

    lax.fori_loop(0, breadth // WIN, per_pair, 0)

    def add_from(held, labels, at):
        step = 16
        marks = [labels[at + c][:1] for c in range(CAP)]
        masks = [[jnp.broadcast_to(jnp.where(mark == s, 1.0, 0.0), (step, LANE)) for mark in marks] for s in range(height // edge * wide)]

        def body(r, carry):
            inside = pl.ds(pl.multiple_of(r * step, step), step)
            for lane in range(0, edge, LANE):
                pieces = [held[at + c, inside, lane : lane + LANE].astype(F32) for c in range(CAP)]
                for s in range(height // edge * wide):
                    rows = pl.ds(pl.multiple_of(s // wide * edge + r * step, step), step)
                    columns = slice(s % wide * edge + lane, s % wide * edge + lane + LANE)
                    value = total[rows, columns]
                    for c in range(CAP):
                        value = value + masks[s][c] * pieces[c]
                    total[rows, columns] = value
            return carry

        lax.fori_loop(0, edge // step, body, 0)

    add_from(outgoing, labels_out, me * CAP)
    for peer in peers:
        theirs = pl.ds(peer * CAP, CAP)
        pltpu.make_async_copy(labels_in.at[theirs], labels_in.at[theirs], label_recv.at[peer]).wait()
        pltpu.make_async_copy(arrived.at[theirs], arrived.at[theirs], block_recv.at[peer]).wait()
        add_from(arrived, labels_in, peer * CAP)
    shift_into(
        lambda rows, t: total[rows, t * LANE : (t + 1) * LANE],
        difference, height, breadth // LANE, 32,
    )
    for copy in row_copies + copies:
        copy.wait_send()


def filter_kernel(halves, difference, column_rows, row_rows, out, column_tables, row_tables, smooth):
    height = difference.shape[0]
    count = column_rows.shape[0]
    pair = pl.program_id(0)

    @pl.when(pair == 0)
    def _():
        build_tables(column_rows, row_rows, column_tables, row_tables, count, *halves)
        clear_edges(smooth, count, height)

    columns_pass(difference, column_tables, smooth, pair, count, height)
    for r in range(height // LANE):
        out[r * LANE : (r + 1) * LANE, :] = rows_pass(smooth, row_tables, count, r)


def padded(taps, flip):
    taps = taps.astype(F32)
    if flip:
        taps = taps[:, ::-1]
    lead = (HALF - taps.shape[1] // 2) % 8
    return jnp.pad(taps, ((0, 0), (lead, WIN - lead - taps.shape[1])))


SMEM = pl.BlockSpec(memory_space=pltpu.SMEM)
VMEM = pl.BlockSpec(memory_space=pltpu.VMEM)
ANY = pl.BlockSpec(memory_space=pl.ANY)


def stencil_scratch(count, height, breadth):
    return [
        pltpu.VMEM((height, breadth + LANE), BF16),
        pltpu.VMEM((WIN, count * LANE), BF16),
        pltpu.VMEM((count, LANE, WIN), BF16),
        pltpu.VMEM((count, height + 2 * HALF, WIN), BF16),
    ]


def per_device(blocks, block_patch, block_slot, block_count, template, basis_rows, basis_cols, coeffs, psf_rows, psf_cols):
    n_patch = lax.axis_size("patch")
    n_visit = lax.axis_size("visit")
    local_rows, breadth = template.shape[1:]
    height = local_rows * n_visit
    entries, edge = blocks.shape[2:4]
    places = n_patch * CAP
    scaled = (coeffs[0][:, None] * basis_cols).astype(BF16)
    count = basis_rows.shape[0]
    dma = pltpu.SemaphoreType.DMA
    difference = pl.pallas_call(
        functools.partial(
            exchange_kernel, n_patch, n_visit, (basis_rows.shape[1] // 2, basis_cols.shape[1] // 2)
        ),
        out_shape=jax.ShapeDtypeStruct((height, breadth + LANE), BF16),
        in_specs=[SMEM, SMEM, SMEM, ANY, ANY, VMEM, VMEM],
        out_specs=VMEM,
        scratch_shapes=[
            pltpu.VMEM((entries, edge, edge), BF16),
            pltpu.VMEM((places, edge, edge), BF16),
            pltpu.VMEM((places, edge, edge), BF16),
            pltpu.VMEM((places, 8, LANE), jnp.int32),
            pltpu.VMEM((places, 8, LANE), jnp.int32),
            pltpu.VMEM((height, breadth), BF16),
            pltpu.VMEM((height, breadth), F32),
        ]
        + stencil_scratch(count, height, breadth)
        + [
            dma(()),
            dma(()),
            dma((n_patch - 1,)),
            dma((n_patch,)),
            dma((n_patch - 1,)),
            dma((n_patch,)),
            dma((n_visit - 1,)),
            dma((n_visit,)),
        ],
        compiler_params=pltpu.CompilerParams(
            collective_id=0, has_side_effects=True, vmem_limit_bytes=VMEM_LIMIT
        ),
    )(
        block_patch.reshape(entries), block_slot.reshape(entries), block_count.reshape(1),
        blocks[0, 0], template[0], padded(basis_rows, True), padded(scaled, False),
    )
    psf_count = psf_rows.shape[1]
    filtered = pl.pallas_call(
        functools.partial(filter_kernel, (psf_rows.shape[2] // 2, psf_cols.shape[2] // 2)),
        out_shape=jax.ShapeDtypeStruct((height, breadth), F32),
        grid=(breadth // WIN,),
        in_specs=[
            pl.BlockSpec((height, breadth + LANE), lambda i: (0, 0)),
            pl.BlockSpec((psf_count, WIN), lambda i: (0, 0)),
            pl.BlockSpec((psf_count, WIN), lambda i: (0, 0)),
        ],
        out_specs=pl.BlockSpec((height, WIN), lambda i: (0, i)),
        scratch_shapes=stencil_scratch(psf_count, height, breadth)[1:],
    )(difference, padded(psf_rows[0], True), padded(psf_cols[0], False))
    return filtered[None, None]


def solution(mesh):
    return jax.shard_map(
        per_device,
        mesh=mesh,
        in_specs=(
            P("patch", "visit", None, None, None),
            P("patch", "visit", None, None),
            P("patch", "visit", None),
            P("patch", "visit"),
            P("patch", "visit", None),
            P(),
            P(),
            P("visit", None),
            P("visit", None, None),
            P("visit", None, None),
        ),
        out_specs=P("patch", "visit", None, None),
        check_vma=False,
    )
```

time: 144 us -> 70.2 us (0.49)
  Pallas kernels: 89.5 us -> 63.6 us
  waiting for transfers between devices: 22.5 us -> 0 us
  blocking collectives: 11.7 us -> 0 us
  starting transfers between devices: 8.24 us -> 0 us
  local copies, waits for them, and re-layouts: 8.78 us -> 2.18 us
    pallas_call x3 -> x2, Pallas kernels: 89.5 us -> 63.6 us  [the longest x1 58.9 us: per_device(): pl.pallas_call(functools.partial(exchange_kernel, n_patch, n_visit, (basi...]
    all_to_all x1 -> x0, waiting for transfers between devices: 17.7 us -> none  [per_device(): lax.all_to_all(outgoing, 'patch', split_axis=0, concat_axis=0, tiled=True)]
    all_to_all x1 -> x0, blocking collectives: 11.7 us -> none  [per_device(): lax.all_to_all(labels, 'patch', split_axis=0, concat_axis=0, tiled=True)]
    ppermute x3 -> x0, waiting for transfers between devices: 4.82 us -> none  [per_device(): lax.ppermute(template[0], 'visit', [(d, (d + hop) % n_visit) for d in ran...]
    ppermute x3 -> x0, starting transfers between devices: 4.5 us -> none  [per_device(): lax.ppermute(template[0], 'visit', [(d, (d + hop) % n_visit) for d in ran...]
    all_to_all x1 -> x0, starting transfers between devices: 3.75 us -> none  [per_device(): lax.all_to_all(outgoing, 'patch', split_axis=0, concat_axis=0, tiled=True)]
    dynamic_update_slice x4 -> x0, local copies, waits for them, and re-layouts: 2.94 us -> none  [the longest x3 2.91 us: per_device(): lax.dynamic_update_slice(whole, moved, ((me + n_visit - hop) % n_visit *...]
    unnamed x16 -> x0, local copies, waits for them, and re-layouts: 2.33 us -> none
  transfers between devices with their start and end apart: 4 -> 0, of which waited for: 3 -> 0; matrix products, arithmetic and copies ran while one was open for 5% -> 0% of each run, Pallas kernels for 9% -> 0%
where the time goes in v2:
time: 70.2 us; the launch traced here: 69.8 us
  Pallas kernels  63.6 us (91%)
  other arithmetic  3.39 us (5%)
  local copies, waits for them, and re-layouts  2.18 us (3%)
    pallas_call x1, Pallas kernels, per_device(): pl.pallas_call(functools.partial(exchange_kernel, n_patch, n_visit, (basi...  58.9 us
    pallas_call x1, Pallas kernels, per_device(): pl.pallas_call(functools.partial(filter_kernel, (psf_rows.shape[2] // 2,...  4.67 us
    pad x2, other arithmetic, padded(): return jnp.pad(taps, ((0, 0), (lead, WIN - lead - taps.shape[1])))  1.97 us

profile of v2, /device:TPU:0, one launch (start us, length us, event | category | flops | bytes accessed | tf_op | source)
XLA Modules:
  0.0 69.8 jit_solution(2346508113286739066)
XLA Ops:
  0.7 0.7 bitcast_convert_fusion
  1.3 0.1 rev.7
  1.4 0.6 pad.21.column_rows
  2.0 1.3 %pad_convert_fusion.1.row_rows = f32[2,256]{1,0:T(2,128)} fusion(bf16[2,25]{1,0:T(2,128)(2,1)} %bitcast.16), kind=kLoop, calls=%fused_computation.2 | loop fusion | flops 512 | bytes 2148 | tf_op jit(solution)/shard_map/jit(_pad)/pad | solution.py:238
  3.3 0.8 %multiply_convert_fusion = bf16[9,21]{1,0:T(8,128)(2,1)S(1)} fusion(f32[9,21]{1,0:T(8,128)} %param.16, f32[9]{0:T(128)} %bitcast.17), kind=kLoop, calls=%fused_computation.1 | loop fusion | flops 378 | bytes 1170 | tf_op jit(solution)/shard_map/convert_element_type | solution.py:262
  4.1 0.8 %rev.6 = f32[9,21]{1,0:T(8,128)S(1)} reverse(bf16[9,21]{1,0:T(8,128)(2,1)} %param.15), dimensions={1} | reverse | bytes 1134 | tf_op jit(solution)/shard_map/rev | solution.py:236
  4.9 0.7 pad.18.column_rows
  5.6 0.7 pad_convert_fusion.row_rows
  6.2 58.9 %shard_map.100.difference = bf16[512,1152]{1,0:T(8,128)(2,1)} custom-call(s32[16]{0:T(128)} %bitcast.14, s32[16]{0:T(128)} %bitcast.15, s32[1]{0:T(128)} %bitcast.11.live, bf16[16,256,256]{2,1,0:T(8,128)(2,1)} %bitcast.12, bf16[128,1024]{1,0:T(8,128)(2,1)} %bitcast.13, f32[9,256]{1,0:T(8,128)} %pad.18.column_rows, f32[9,256]{1,0:T(8,128)} %pad_convert_fusion.row_rows), custom_call_target="tpu_custom_call" | custom-call | tf_op jit(solution)/shard_map/pallas_call | solution.py:265
  65.2 4.7 %shard_map.101 = f32[512,1024]{1,0:T(8,128)} custom-call(bf16[512,1152]{1,0:T(8,128)(2,1)} %shard_map.100.difference, f32[2,256]{1,0:T(2,128)} %pad.21.column_rows, f32[2,256]{1,0:T(2,128)} %pad_convert_fusion.1.row_rows), custom_call_target="tpu_custom_call" | custom-call | tf_op jit(solution)/shard_map/pallas_call | solution.py:300

commit v3 on v2

--- a/solution.py
+++ b/solution.py
@@ -16,14 +16,18 @@
 VMEM_LIMIT = 56 * 1024 * 1024
 
 
-def column_table(row, half_len):
-    wide = jnp.broadcast_to(row, (WIN, WIN))
-    return pltpu.roll(wide, (WIN - HALF - half_len) // 8 * 8, 1, stride=1, stride_axis=0)[:, :LANE].astype(BF16)
-
-
-def row_table(row, half_len):
+def toeplitz(row, half_len):
     wide = jnp.broadcast_to(row, (LANE, WIN))
-    return pltpu.roll(wide, (HALF - half_len) // 8 * 8, 1, stride=1, stride_axis=0).astype(BF16)
+    return pltpu.roll(wide, (HALF - half_len) // 8 * 8, 1, stride=1, stride_axis=0)
+
+
+def spread(taps, staged):
+    count, length = taps.shape
+    staged[...] = jnp.zeros(staged.shape, F32)
+    staged[:count, :length] = taps
+    lead = (HALF - length // 2) % 8
+    if lead:
+        staged[...] = pltpu.roll(staged[...], lead, 1)
 
 
 def shift_into(load_tile, shifted, height, tiles, step):
@@ -64,10 +68,14 @@
     return total
 
 
-def build_tables(column_rows, row_rows, column_tables, row_tables, count, half_c, half_r):
-    for k in range(count):
-        column_tables[:, k * LANE : (k + 1) * LANE] = column_table(column_rows[k : k + 1, :], half_c)
-        row_tables[k] = row_table(row_rows[k : k + 1, :], half_r)
+def build_tables(column_taps, row_taps, column_tables, row_tables, staged):
+    spread(column_taps, staged)
+    for k in range(column_taps.shape[0]):
+        table = toeplitz(staged[k : k + 1, :], column_taps.shape[1] // 2)
+        column_tables[:, k * LANE : (k + 1) * LANE] = table.T.astype(BF16)
+    spread(row_taps, staged)
+    for k in range(row_taps.shape[0]):
+        row_tables[k] = toeplitz(staged[k : k + 1, :], row_taps.shape[1] // 2).astype(BF16)
 
 
 def clear_edges(smooth, count, height):
@@ -77,10 +85,10 @@
 
 
 def exchange_kernel(
-    n_patch, n_visit, halves,
-    patch, slot, live, blocks, template, column_rows, row_rows,
-    difference,
-    raw, outgoing, arrived, labels_out, labels_in, whole, total, shifted, column_tables, row_tables, smooth,
+    n_patch, n_visit,
+    patch, slot, live, coeffs, blocks, template, basis_rows, basis_cols, psf_rows, psf_cols,
+    difference, psf_column_tables, psf_row_tables,
+    staged, raw, outgoing, arrived, labels_out, labels_in, whole, total, shifted, column_tables, row_tables, smooth,
     load_sem, own_sem, block_send, block_recv, label_send, label_recv, rows_send, rows_recv,
 ):
     me = lax.axis_index("patch")
@@ -88,10 +96,15 @@
     local_rows, breadth = template.shape
     height = local_rows * n_visit
     entries, edge = blocks.shape[:2]
-    count = column_rows.shape[0]
+    count = basis_rows.shape[0]
     wide = breadth // edge
-    turn = 1 - 2 * (me // (n_patch // 2))
-    peers = [lax.rem(me + turn * hop + n_patch, n_patch) for hop in range(1, n_patch)]
+    chips = n_patch // 2
+    chip, core = me // 2, lax.rem(me, 2)
+    turn = 1 - 2 * (me // chips)
+    peers = [2 * chip + 1 - core]
+    for hop in range(chips - 1, 0, -1):
+        there = 2 * lax.rem(chip + turn * hop + chips, chips)
+        peers += [there + core, there + 1 - core]
     visits = [lax.rem(my_visit + hop, n_visit) for hop in range(1, n_visit)]
 
     load = pltpu.make_async_copy(blocks, raw, load_sem)
@@ -112,7 +125,7 @@
         for before in range(i):
             earlier = earlier + jnp.where(targets[before] == targets[i], 1, 0)
         place_of.append(targets[i] * CAP + earlier)
-    marks = [jnp.where(i < live[0], slot[i] + 1, 0) for i in range(entries)]
+    marks = [jnp.where(i < live[0, 0], slot[i] + 1, 0) for i in range(entries)]
     load.wait()
 
     def pack(d, carry):
@@ -157,7 +170,11 @@
     for copy in copies:
         copy.start()
 
-    build_tables(column_rows, row_rows, column_tables, row_tables, count, *halves)
+    scaled = jnp.concatenate(
+        [(coeffs[0, k] * basis_cols[k : k + 1, :]).astype(BF16).astype(F32) for k in range(count)], axis=0
+    )
+    build_tables(basis_rows[...].astype(F32), scaled, column_tables, row_tables, staged)
+    build_tables(psf_rows[0].astype(F32), psf_cols[0].astype(F32), psf_column_tables, psf_row_tables, staged)
     clear_edges(smooth, count, height)
     own.wait()
     for visit in visits:
@@ -215,27 +232,18 @@
         copy.wait_send()
 
 
-def filter_kernel(halves, difference, column_rows, row_rows, out, column_tables, row_tables, smooth):
+def filter_kernel(difference, column_tables, row_tables, out, smooth):
     height = difference.shape[0]
-    count = column_rows.shape[0]
+    count = row_tables.shape[0]
     pair = pl.program_id(0)
 
     @pl.when(pair == 0)
     def _():
-        build_tables(column_rows, row_rows, column_tables, row_tables, count, *halves)
         clear_edges(smooth, count, height)
 
     columns_pass(difference, column_tables, smooth, pair, count, height)
     for r in range(height // LANE):
         out[r * LANE : (r + 1) * LANE, :] = rows_pass(smooth, row_tables, count, r)
-
-
-def padded(taps, flip):
-    taps = taps.astype(F32)
-    if flip:
-        taps = taps[:, ::-1]
-    lead = (HALF - taps.shape[1] // 2) % 8
-    return jnp.pad(taps, ((0, 0), (lead, WIN - lead - taps.shape[1])))
 
 
 SMEM = pl.BlockSpec(memory_space=pltpu.SMEM)
@@ -259,17 +267,22 @@
     height = local_rows * n_visit
     entries, edge = blocks.shape[2:4]
     places = n_patch * CAP
-    scaled = (coeffs[0][:, None] * basis_cols).astype(BF16)
     count = basis_rows.shape[0]
+    psf_count = psf_rows.shape[1]
     dma = pltpu.SemaphoreType.DMA
-    difference = pl.pallas_call(
+    difference, psf_column_tables, psf_row_tables = pl.pallas_call(
         functools.partial(
-            exchange_kernel, n_patch, n_visit, (basis_rows.shape[1] // 2, basis_cols.shape[1] // 2)
+            exchange_kernel, n_patch, n_visit
         ),
-        out_shape=jax.ShapeDtypeStruct((height, breadth + LANE), BF16),
-        in_specs=[SMEM, SMEM, SMEM, ANY, ANY, VMEM, VMEM],
-        out_specs=VMEM,
+        out_shape=(
+            jax.ShapeDtypeStruct((height, breadth + LANE), BF16),
+            jax.ShapeDtypeStruct((WIN, psf_count * LANE), BF16),
+            jax.ShapeDtypeStruct((psf_count, LANE, WIN), BF16),
+        ),
+        in_specs=[SMEM] * 4 + [ANY] * 2 + [VMEM] * 4,
+        out_specs=(VMEM,) * 3,
         scratch_shapes=[
+            pltpu.VMEM((pl.cdiv(max(count, psf_count), 8) * 8, WIN), F32),
             pltpu.VMEM((entries, edge, edge), BF16),
             pltpu.VMEM((places, edge, edge), BF16),
             pltpu.VMEM((places, edge, edge), BF16),
@@ -293,22 +306,21 @@
             collective_id=0, has_side_effects=True, vmem_limit_bytes=VMEM_LIMIT
         ),
     )(
-        block_patch.reshape(entries), block_slot.reshape(entries), block_count.reshape(1),
-        blocks[0, 0], template[0], padded(basis_rows, True), padded(scaled, False),
-    )
-    psf_count = psf_rows.shape[1]
+        block_patch.reshape(entries), block_slot.reshape(entries), block_count, coeffs,
+        blocks[0, 0], template[0], basis_rows, basis_cols, psf_rows, psf_cols,
+    )
     filtered = pl.pallas_call(
-        functools.partial(filter_kernel, (psf_rows.shape[2] // 2, psf_cols.shape[2] // 2)),
+        filter_kernel,
         out_shape=jax.ShapeDtypeStruct((height, breadth), F32),
         grid=(breadth // WIN,),
         in_specs=[
             pl.BlockSpec((height, breadth + LANE), lambda i: (0, 0)),
-            pl.BlockSpec((psf_count, WIN), lambda i: (0, 0)),
-            pl.BlockSpec((psf_count, WIN), lambda i: (0, 0)),
+            pl.BlockSpec((WIN, psf_count * LANE), lambda i: (0, 0)),
+            pl.BlockSpec((psf_count, LANE, WIN), lambda i: (0, 0, 0)),
         ],
         out_specs=pl.BlockSpec((height, WIN), lambda i: (0, i)),
-        scratch_shapes=stencil_scratch(psf_count, height, breadth)[1:],
-    )(difference, padded(psf_rows[0], True), padded(psf_cols[0], False))
+        scratch_shapes=stencil_scratch(psf_count, height, breadth)[3:],
+    )(difference, psf_column_tables, psf_row_tables)
     return filtered[None, None]
 
 

time: 70.2 us -> 60.7 us (0.86)
  the two profiles are of different devices: /device:TPU:0 before, /device:TPU:9 now
where the time goes in v3:
time: 60.7 us; the launch traced here: 60.5 us
  Pallas kernels  59.8 us (99%)
  between operations  0.66 us (1%)
    pallas_call x1, Pallas kernels, per_device(): pl.pallas_call(functools.partial(exchange_kernel, n_patch, n_visit), out_...  55.2 us
    pallas_call x1, Pallas kernels, per_device(): pl.pallas_call(filter_kernel, out_shape=jax.ShapeDtypeStruct((height, bre...  4.64 us

profile of v3, /device:TPU:9, one launch (start us, length us, event | category | flops | bytes accessed | tf_op | source)
XLA Modules:
  0.0 60.5 jit_solution(2384267475511273667)
XLA Ops:
  0.7 55.2 %shard_map.100 = (bf16[512,1152]{1,0:T(8,128)(2,1)}, bf16[256,256]{1,0:T(8,128)(2,1)}, bf16[2,128,256]{2,1,0:T(8,128)(2,1)}) custom-call(s32[16]{0:T(128)} %bitcast.7, s32[16]{0:T(128)} %bitcast.8, s32[1,1]{1,0:T(1,128)S(6)} %copy.11.live, f32[1,9]{1,0:T(1,128)} %coeffs.1, bf16[16,256,256]{2,1,0:T(8,128)(2,1)} %bitcast.5, bf16[128,1024]{1,0:T(8,128)(2,1)} %bitcast.6, ...), custom_call_target="tpu_custom_call" | custom-call | tf_op jit(solution)/shard_map/pallas_call | solution.py:273
  55.8 4.6 %shard_map.101 = f32[512,1024]{1,0:T(8,128)} custom-call(bf16[512,1152]{1,0:T(8,128)(2,1)} %get-tuple-element.8.difference, bf16[256,256]{1,0:T(8,128)(2,1)} %get-tuple-element.9.column_tables, bf16[2,128,256]{2,1,0:T(8,128)(2,1)} %get-tuple-element.10.row_tables), custom_call_target="tpu_custom_call" | custom-call | tf_op jit(solution)/shard_map/pallas_call | solution.py:312

commit v4 on v3

--- a/solution.py
+++ b/solution.py
@@ -10,10 +10,11 @@
 CAP = 2
 LANE = 128
 HALF = 64
+EDGE = 16
 WIN = 256
 F32 = jnp.float32
 BF16 = jnp.bfloat16
-VMEM_LIMIT = 56 * 1024 * 1024
+VMEM_LIMIT = 32 * 1024 * 1024
 
 
 def toeplitz(row, half_len):
@@ -45,7 +46,7 @@
     lax.fori_loop(0, height // step, body, 0)
 
 
-def columns_pass(shifted, tables, smooth, pair, count, height):
+def columns_pass(shifted, tables, smooth, pair, count, height, margin=HALF):
     for side in range(2):
         start = pl.multiple_of((2 * pair + side) * LANE, LANE)
         window = shifted[:, pl.ds(start, WIN)]
@@ -55,7 +56,7 @@
                 window, tables[:, group * LANE : (group + taken) * LANE], preferred_element_type=F32
             ).astype(BF16)
             for k in range(taken):
-                smooth[group + k, HALF : HALF + height, side * LANE : (side + 1) * LANE] = got[
+                smooth[group + k, margin : margin + height, side * LANE : (side + 1) * LANE] = got[
                     :, k * LANE : (k + 1) * LANE
                 ]
 
@@ -66,6 +67,20 @@
     for k in range(count):
         total = total + jnp.dot(tables[k], smooth[k, pl.ds(start, WIN), :], preferred_element_type=F32)
     return total
+
+
+def band(row, half_len):
+    parts = []
+    for start in range(0, WIN + 2 * EDGE, EDGE):
+        shift = (start - EDGE - half_len - (HALF - half_len) % 8) % WIN
+        wide = jnp.broadcast_to(row, (EDGE, WIN))
+        rolled = pltpu.roll(wide, shift, 1, stride=1, stride_axis=0)
+        offset = (
+            lax.broadcasted_iota(jnp.int32, (EDGE, WIN), 1)
+            - lax.broadcasted_iota(jnp.int32, (EDGE, WIN), 0) - start + EDGE
+        )
+        parts.append(jnp.where((offset >= -half_len) & (offset <= half_len), rolled, 0.0))
+    return parts
 
 
 def build_tables(column_taps, row_taps, column_tables, row_tables, staged):
@@ -75,7 +90,12 @@
         column_tables[:, k * LANE : (k + 1) * LANE] = table.T.astype(BF16)
     spread(row_taps, staged)
     for k in range(row_taps.shape[0]):
-        row_tables[k] = toeplitz(staged[k : k + 1, :], row_taps.shape[1] // 2).astype(BF16)
+        half_len = row_taps.shape[1] // 2
+        if row_tables.shape[1] == LANE:
+            row_tables[k] = toeplitz(staged[k : k + 1, :], half_len).astype(BF16)
+        else:
+            for part, rows in enumerate(band(staged[k : k + 1, :], half_len)):
+                row_tables[k, part * EDGE : (part + 1) * EDGE, :] = rows.astype(BF16)
 
 
 def clear_edges(smooth, count, height):
@@ -86,9 +106,9 @@
 
 def exchange_kernel(
     n_patch, n_visit,
-    patch, slot, live, coeffs, blocks, template, basis_rows, basis_cols, psf_rows, psf_cols,
+    live, patch_in, slot_in, coeffs_in, basis_rows_in, basis_cols_in, psf_rows_in, psf_cols_in, blocks, template,
     difference, psf_column_tables, psf_row_tables,
-    staged, raw, outgoing, arrived, labels_out, labels_in, whole, total, shifted, column_tables, row_tables, smooth,
+    patch, slot, coeffs, basis_rows, basis_cols, psf_rows, psf_cols, small_sems, sources, staged, raw, outgoing, arrived, labels_out, labels_in, whole, total, shifted, column_tables, row_tables, smooth,
     load_sem, own_sem, block_send, block_recv, label_send, label_recv, rows_send, rows_recv,
 ):
     me = lax.axis_index("patch")
@@ -107,6 +127,18 @@
         peers += [there + core, there + 1 - core]
     visits = [lax.rem(my_visit + hop, n_visit) for hop in range(1, n_visit)]
 
+    small = [
+        pltpu.make_async_copy(source, held, small_sems.at[i])
+        for i, (source, held) in enumerate(
+            (
+                (patch_in, patch), (slot_in, slot), (coeffs_in, coeffs),
+                (basis_rows_in, basis_rows), (basis_cols_in, basis_cols),
+                (psf_rows_in, psf_rows), (psf_cols_in, psf_cols),
+            )
+        )
+    ]
+    for copy in small:
+        copy.start()
     load = pltpu.make_async_copy(blocks, raw, load_sem)
     load.start()
     my_rows = pl.ds(pl.multiple_of(my_visit * local_rows, local_rows), local_rows)
@@ -118,6 +150,8 @@
     for visit in visits:
         pl.semaphore_signal(barrier, inc=1, device_id={"visit": visit}, device_id_type=pl.DeviceIdType.MESH)
 
+    for copy in small[:2]:
+        copy.wait()
     targets = [patch[i] for i in range(entries)]
     place_of = []
     for i in range(entries):
@@ -126,16 +160,22 @@
             earlier = earlier + jnp.where(targets[before] == targets[i], 1, 0)
         place_of.append(targets[i] * CAP + earlier)
     marks = [jnp.where(i < live[0, 0], slot[i] + 1, 0) for i in range(entries)]
-    load.wait()
-
-    def pack(d, carry):
+
+    def find(d, carry):
         source = jnp.int32(0)
         label = jnp.int32(-1)
         for i in range(entries):
             source = source + jnp.where(place_of[i] == d, i, 0)
             label = label + jnp.where(place_of[i] == d, marks[i], 0)
-        outgoing[d] = raw[source]
+        sources[d] = source
         labels_out[d] = jnp.full((8, LANE), label, jnp.int32)
+        return carry
+
+    lax.fori_loop(0, n_patch * CAP, find, 0)
+    load.wait()
+
+    def pack(d, carry):
+        outgoing[d] = raw[sources[d]]
         return carry
 
     lax.fori_loop(0, n_patch * CAP, pack, 0)
@@ -170,6 +210,8 @@
     for copy in copies:
         copy.start()
 
+    for copy in small[2:]:
+        copy.wait()
     scaled = jnp.concatenate(
         [(coeffs[0, k] * basis_cols[k : k + 1, :]).astype(BF16).astype(F32) for k in range(count)], axis=0
     )
@@ -200,20 +242,23 @@
 
     def add_from(held, labels, at):
         step = 16
-        marks = [labels[at + c][:1] for c in range(CAP)]
-        masks = [[jnp.broadcast_to(jnp.where(mark == s, 1.0, 0.0), (step, LANE)) for mark in marks] for s in range(height // edge * wide)]
+        marks = [labels[at + c] for c in range(CAP)]
+        masks = [[jnp.where(mark == s, 1.0, 0.0) for mark in marks] for s in range(height // edge * wide)]
 
         def body(r, carry):
             inside = pl.ds(pl.multiple_of(r * step, step), step)
             for lane in range(0, edge, LANE):
-                pieces = [held[at + c, inside, lane : lane + LANE].astype(F32) for c in range(CAP)]
+                pieces = [
+                    held[at + c, inside, lane : lane + LANE].astype(F32).reshape(step // 8, 8, LANE)
+                    for c in range(CAP)
+                ]
                 for s in range(height // edge * wide):
                     rows = pl.ds(pl.multiple_of(s // wide * edge + r * step, step), step)
                     columns = slice(s % wide * edge + lane, s % wide * edge + lane + LANE)
-                    value = total[rows, columns]
+                    value = total[rows, columns].reshape(step // 8, 8, LANE)
                     for c in range(CAP):
-                        value = value + masks[s][c] * pieces[c]
-                    total[rows, columns] = value
+                        value = value + masks[s][c][None] * pieces[c]
+                    total[rows, columns] = value.reshape(step, LANE)
             return carry
 
         lax.fori_loop(0, edge // step, body, 0)
@@ -236,19 +281,28 @@
     height = difference.shape[0]
     count = row_tables.shape[0]
     pair = pl.program_id(0)
-
-    @pl.when(pair == 0)
-    def _():
-        clear_edges(smooth, count, height)
-
-    columns_pass(difference, column_tables, smooth, pair, count, height)
-    for r in range(height // LANE):
-        out[r * LANE : (r + 1) * LANE, :] = rows_pass(smooth, row_tables, count, r)
+    columns_pass(difference, column_tables, smooth, pair, count, height, 0)
+    chunks = height // WIN
+    for chunk in range(chunks):
+        first, last = chunk == 0, chunk == chunks - 1
+        low = EDGE if first else 0
+        high = WIN + EDGE if last else WIN + 2 * EDGE
+        got = jnp.zeros((high - low, WIN), F32)
+        for k in range(count):
+            got = got + jnp.dot(
+                row_tables[k, low:high, :], smooth[k, chunk * WIN : (chunk + 1) * WIN, :], preferred_element_type=F32
+            )
+        start = chunk * WIN - EDGE + low
+        if first:
+            out[start : start + high - low, :] = got
+        else:
+            out[start : start + 2 * EDGE, :] = out[start : start + 2 * EDGE, :] + got[: 2 * EDGE]
+            out[start + 2 * EDGE : start + high - low, :] = got[2 * EDGE :]
 
 
 SMEM = pl.BlockSpec(memory_space=pltpu.SMEM)
+HBM = pl.BlockSpec(memory_space=pltpu.HBM)
 VMEM = pl.BlockSpec(memory_space=pltpu.VMEM)
-ANY = pl.BlockSpec(memory_space=pl.ANY)
 
 
 def stencil_scratch(count, height, breadth):
@@ -277,11 +331,20 @@
         out_shape=(
             jax.ShapeDtypeStruct((height, breadth + LANE), BF16),
             jax.ShapeDtypeStruct((WIN, psf_count * LANE), BF16),
-            jax.ShapeDtypeStruct((psf_count, LANE, WIN), BF16),
+            jax.ShapeDtypeStruct((psf_count, WIN + 2 * EDGE, WIN), BF16),
         ),
-        in_specs=[SMEM] * 4 + [ANY] * 2 + [VMEM] * 4,
+        in_specs=[SMEM] + [HBM] * 9,
         out_specs=(VMEM,) * 3,
         scratch_shapes=[
+            pltpu.SMEM((entries,), jnp.int32),
+            pltpu.SMEM((entries,), jnp.int32),
+            pltpu.SMEM(coeffs.shape, F32),
+            pltpu.VMEM(basis_rows.shape, BF16),
+            pltpu.VMEM(basis_cols.shape, F32),
+            pltpu.VMEM(psf_rows.shape, BF16),
+            pltpu.VMEM(psf_cols.shape, BF16),
+            dma((7,)),
+            pltpu.SMEM((places,), jnp.int32),
             pltpu.VMEM((pl.cdiv(max(count, psf_count), 8) * 8, WIN), F32),
             pltpu.VMEM((entries, edge, edge), BF16),
             pltpu.VMEM((places, edge, edge), BF16),
@@ -306,8 +369,14 @@
             collective_id=0, has_side_effects=True, vmem_limit_bytes=VMEM_LIMIT
         ),
     )(
-        block_patch.reshape(entries), block_slot.reshape(entries), block_count, coeffs,
-        blocks[0, 0], template[0], basis_rows, basis_cols, psf_rows, psf_cols,
+        block_count,
+        *(
+            pltpu.with_memory_space_constraint(value, pltpu.HBM)
+            for value in (
+                block_patch.reshape(entries), block_slot.reshape(entries), coeffs,
+                basis_rows, basis_cols, psf_rows, psf_cols, blocks[0, 0], template[0],
+            )
+        )
     )
     filtered = pl.pallas_call(
         filter_kernel,
@@ -316,10 +385,11 @@
         in_specs=[
             pl.BlockSpec((height, breadth + LANE), lambda i: (0, 0)),
             pl.BlockSpec((WIN, psf_count * LANE), lambda i: (0, 0)),
-            pl.BlockSpec((psf_count, LANE, WIN), lambda i: (0, 0, 0)),
+            pl.BlockSpec((psf_count, WIN + 2 * EDGE, WIN), lambda i: (0, 0, 0)),
         ],
         out_specs=pl.BlockSpec((height, WIN), lambda i: (0, i)),
-        scratch_shapes=stencil_scratch(psf_count, height, breadth)[3:],
+        scratch_shapes=[pltpu.VMEM((psf_count, height, WIN), BF16)],
+        compiler_params=pltpu.CompilerParams(vmem_limit_bytes=16 * 1024 * 1024),
     )(difference, psf_column_tables, psf_row_tables)
     return filtered[None, None]
 

time: 60.7 us -> 58.1 us (0.957)
  Pallas kernels: 59.8 us -> 57.2 us
    pallas_call x1, Pallas kernels: 55.2 us -> 53.3 us  [per_device(): pl.pallas_call(functools.partial(exchange_kernel, n_patch, n_visit), out_...]
    pallas_call x1, Pallas kernels: 4.64 us -> 3.96 us  [per_device(): pl.pallas_call(filter_kernel, out_shape=jax.ShapeDtypeStruct((height, bre...]
where the time goes in v4:
time: 58.1 us; the launch traced here: 57.9 us
  Pallas kernels  57.2 us (98%)
  between operations  0.66 us (1%)
    pallas_call x1, Pallas kernels, per_device(): pl.pallas_call(functools.partial(exchange_kernel, n_patch, n_visit), out_...  53.3 us
    pallas_call x1, Pallas kernels, per_device(): pl.pallas_call(filter_kernel, out_shape=jax.ShapeDtypeStruct((height, bre...  3.96 us

profile of v4, /device:TPU:9, one launch (start us, length us, event | category | flops | bytes accessed | tf_op | source)
XLA Modules:
  0.0 57.9 jit_solution(13796528198469280917)
XLA Ops:
  0.7 53.3 %shard_map.100 = (bf16[512,1152]{1,0:T(8,128)(2,1)S(1)}, bf16[256,256]{1,0:T(8,128)(2,1)S(1)}, bf16[2,288,256]{2,1,0:T(8,128)(2,1)S(1)}) custom-call(s32[1,1]{1,0:T(1,128)S(6)} %copy.11.live, s32[16]{0:T(128)} %bitcast.7, s32[16]{0:T(128)} %bitcast.8, f32[1,9]{1,0:T(1,128)} %coeffs_in.1, bf16[9,21]{1,0:T(8,128)(2,1)} %basis_rows_in.1, ...), custom_call_target="tpu_custom_call" | custom-call | tf_op jit(solution)/shard_map/pallas_call | solution.py:327
  53.9 4.0 %shard_map.101 = f32[512,1024]{1,0:T(8,128)} custom-call(bf16[512,1152]{1,0:T(8,128)(2,1)S(1)} %get-tuple-element.8.difference, bf16[256,256]{1,0:T(8,128)(2,1)S(1)} %get-tuple-element.9.column_tables, bf16[2,288,256]{2,1,0:T(8,128)(2,1)S(1)} %get-tuple-element.10.row_tables), custom_call_target="tpu_custom_call" | custom-call | tf_op jit(solution)/shard_map/pallas_call | solution.py:381

commit v5 on v4

--- a/solution.py
+++ b/solution.py
@@ -162,16 +162,17 @@
     marks = [jnp.where(i < live[0, 0], slot[i] + 1, 0) for i in range(entries)]
 
     def find(d, carry):
-        source = jnp.int32(0)
-        label = jnp.int32(-1)
-        for i in range(entries):
-            source = source + jnp.where(place_of[i] == d, i, 0)
-            label = label + jnp.where(place_of[i] == d, marks[i], 0)
-        sources[d] = source
-        labels_out[d] = jnp.full((8, LANE), label, jnp.int32)
+        for c in range(CAP):
+            source = jnp.int32(0)
+            label = jnp.int32(-1)
+            for i in range(entries):
+                source = source + jnp.where(place_of[i] == d * CAP + c, i, 0)
+                label = label + jnp.where(place_of[i] == d * CAP + c, marks[i], 0)
+            sources[d * CAP + c] = source
+            labels_out[d, c : c + 1, :] = jnp.full((1, LANE), label, jnp.int32)
         return carry
 
-    lax.fori_loop(0, n_patch * CAP, find, 0)
+    lax.fori_loop(0, n_patch, find, 0)
     load.wait()
 
     def pack(d, carry):
@@ -195,12 +196,12 @@
         theirs = pl.ds(peer * CAP, CAP)
         mine = pl.ds(me * CAP, CAP)
         for source, target, send, recv in (
-            (labels_out, labels_in, label_send, label_recv),
-            (outgoing, arrived, block_send, block_recv),
+            (labels_out.at[peer], labels_in.at[me], label_send, label_recv),
+            (outgoing.at[theirs], arrived.at[mine], block_send, block_recv),
         ):
             copies.append(
                 pltpu.make_async_remote_copy(
-                    src_ref=source.at[theirs], dst_ref=target.at[mine],
+                    src_ref=source, dst_ref=target,
                     send_sem=send.at[hop], recv_sem=recv.at[me],
                     device_id={"patch": peer}, device_id_type=pl.DeviceIdType.MESH,
                 )
@@ -240,10 +241,11 @@
 
     lax.fori_loop(0, breadth // WIN, per_pair, 0)
 
-    def add_from(held, labels, at):
+    def add_from(held, labels, source):
         step = 16
-        marks = [labels[at + c] for c in range(CAP)]
-        masks = [[jnp.where(mark == s, 1.0, 0.0) for mark in marks] for s in range(height // edge * wide)]
+        at = source * CAP
+        marks = [labels[source, c : c + 1, :] for c in range(CAP)]
+        masks = [[jnp.broadcast_to(jnp.where(mark == s, 1.0, 0.0), (8, LANE)) for mark in marks] for s in range(height // edge * wide)]
 
         def body(r, carry):
             inside = pl.ds(pl.multiple_of(r * step, step), step)
@@ -263,12 +265,12 @@
 
         lax.fori_loop(0, edge // step, body, 0)
 
-    add_from(outgoing, labels_out, me * CAP)
+    add_from(outgoing, labels_out, me)
     for peer in peers:
         theirs = pl.ds(peer * CAP, CAP)
-        pltpu.make_async_copy(labels_in.at[theirs], labels_in.at[theirs], label_recv.at[peer]).wait()
+        pltpu.make_async_copy(labels_in.at[peer], labels_in.at[peer], label_recv.at[peer]).wait()
         pltpu.make_async_copy(arrived.at[theirs], arrived.at[theirs], block_recv.at[peer]).wait()
-        add_from(arrived, labels_in, peer * CAP)
+        add_from(arrived, labels_in, peer)
     shift_into(
         lambda rows, t: total[rows, t * LANE : (t + 1) * LANE],
         difference, height, breadth // LANE, 32,
@@ -349,8 +351,8 @@
             pltpu.VMEM((entries, edge, edge), BF16),
             pltpu.VMEM((places, edge, edge), BF16),
             pltpu.VMEM((places, edge, edge), BF16),
-            pltpu.VMEM((places, 8, LANE), jnp.int32),
-            pltpu.VMEM((places, 8, LANE), jnp.int32),
+            pltpu.VMEM((n_patch, CAP, LANE), jnp.int32),
+            pltpu.VMEM((n_patch, CAP, LANE), jnp.int32),
             pltpu.VMEM((height, breadth), BF16),
             pltpu.VMEM((height, breadth), F32),
         ]

time: 58.1 us -> 56.8 us (0.978)
  Pallas kernels: 57.2 us -> 56 us
    pallas_call x1, Pallas kernels: 53.3 us -> 52.1 us  [per_device(): pl.pallas_call(functools.partial(exchange_kernel, n_patch, n_visit), out_...]
where the time goes in v5:
time: 56.8 us; the launch traced here: 56.7 us
  Pallas kernels  56 us (99%)
  between operations  0.66 us (1%)
    pallas_call x1, Pallas kernels, per_device(): pl.pallas_call(functools.partial(exchange_kernel, n_patch, n_visit), out_...  52.1 us
    pallas_call x1, Pallas kernels, per_device(): pl.pallas_call(filter_kernel, out_shape=jax.ShapeDtypeStruct((height, bre...  3.96 us

profile of v5, /device:TPU:9, one launch (start us, length us, event | category | flops | bytes accessed | tf_op | source)
XLA Modules:
  0.0 56.7 jit_solution(13103572660164010724)
XLA Ops:
  0.7 52.1 %shard_map.100 = (bf16[512,1152]{1,0:T(8,128)(2,1)S(1)}, bf16[256,256]{1,0:T(8,128)(2,1)S(1)}, bf16[2,288,256]{2,1,0:T(8,128)(2,1)S(1)}) custom-call(s32[1,1]{1,0:T(1,128)S(6)} %copy.11.live, s32[16]{0:T(128)} %bitcast.7, s32[16]{0:T(128)} %bitcast.8, f32[1,9]{1,0:T(1,128)} %coeffs_in.1, bf16[9,21]{1,0:T(8,128)(2,1)} %basis_rows_in.1, ...), custom_call_target="tpu_custom_call" | custom-call | tf_op jit(solution)/shard_map/pallas_call | solution.py:329
  52.7 4.0 %shard_map.101 = f32[512,1024]{1,0:T(8,128)} custom-call(bf16[512,1152]{1,0:T(8,128)(2,1)S(1)} %get-tuple-element.8.difference, bf16[256,256]{1,0:T(8,128)(2,1)S(1)} %get-tuple-element.9.column_tables, bf16[2,288,256]{2,1,0:T(8,128)(2,1)S(1)} %get-tuple-element.10.row_tables), custom_call_target="tpu_custom_call" | custom-call | tf_op jit(solution)/shard_map/pallas_call | solution.py:383
